TPU v7x, 1024 devices: a whole 4x8x16 slice. The times are simulated.
1024 devices in a mesh: lon: 128 (over z, y_lo, core), lat: 8 (over y_hi, x).
Axes of the slice: x: 4, y: 8 (y_hi: 2, y_lo: 4; y = y_hi * 4 + y_lo), z: 16, core: 2. Of those that a mesh axis runs over, the one named last changes fastest.
Arguments:
- adjoint_height: float32 [4096, 16384], P('lat', 'lon'), may hold values from -6 to 6
- depth: float32 [4096, 16384], P('lat', 'lon'), may hold values from 0.1 to 1
- wet: int32 [4096, 16384], P('lat', 'lon'), may hold values 0 or 1
- basis_lat: float32 [32, 4096], P(None, 'lat'), may hold values from -1.5 to 1.5
- basis_lon: float32 [32, 16384], P(None, 'lon'), may hold values from -1.5 to 1.5
- tile_owner: int32 [256, 1024], P('lat', 'lon'), may hold values from 0 to 127, as said below
- tile_patch: int32 [256, 1024], P('lat', 'lon'), may hold values from 0 to 255
- tile_count: int32 [256, 1024], P('lat', 'lon'), may hold values from 1 to 32
- prior_patches: float32 [8, 128, 256, 256], P('lat', 'lon'), may hold values from 0 to 11
- prior_subfaults: float32 [32, 32], replicated, may hold values from -0.4 to 1.7
Outputs:
- adjoint_final: float32 [4096, 16384], P('lat', 'lon')
- source_gradient: float32 [4096, 16384], P('lat', 'lon')
Inputs may be any that keep to these rules, and one draw needn't show every extreme that they name: `tile_owner`: within each device's block of tiles no owner is named more than 3 times, and in every latitude band one owner is named exactly 3 times by every device's block.
All inputs are finite; a program needn't handle non-finite values. No bound on the sum of `wet` on one device may be relied on, other than what follows from the above.
Results may differ from a plain program's by a relative error of at most 0.0002.
Values sent between devices are 32-bit elements; how exact they have to be, the bound alone decides.
No kernel may reach another device: no remote copies, remote signals or barrier semaphores. Data moves between devices by JAX's collectives and lax.ppermute only.
A program may use at most 32 MiB of HBM per device.

v0:
```python
import jax
import jax.numpy as jnp
from jax import lax
from jax.sharding import PartitionSpec as P

STEPS = 4
TS = 16
SUB = 32
NPATCH = 256


COURANT = 0.6


def padded(block, sides, width, periodic):
    for axis, dim in sides:
        count = lax.axis_size(axis)
        forward = [(i, i + 1) for i in range(count - 1)]
        if periodic:
            forward.append((count - 1, 0))
        backward = [(target, source) for source, target in forward]
        low = lax.ppermute(
            lax.slice_in_dim(block, block.shape[dim] - width, None, axis=dim), axis, forward
        )
        high = lax.ppermute(lax.slice_in_dim(block, 0, width, axis=dim), axis, backward)
        block = jnp.concatenate([low, block, high], axis=dim)
    return block


def adjoint_step(height, east, north, wet_depth):
    east_new = east[:, :-1] + COURANT * jnp.minimum(wet_depth[:, :-1], wet_depth[:, 1:]) * (
        height[:, 1:] - height[:, :-1]
    )
    north_new = north[:-1, :] + COURANT * jnp.minimum(wet_depth[:-1, :], wet_depth[1:, :]) * (
        height[1:, :] - height[:-1, :]
    )
    height_new = (
        height[1:-1, 1:-1]
        + COURANT * (east_new[1:-1, 1:] - east_new[1:-1, :-1])
        + COURANT * (north_new[1:, 1:-1] - north_new[:-1, 1:-1])
    )
    return (height_new, east_new[1:-1, 1:], north_new[1:, 1:-1])


def widen(fields, rim_width):
    looped = padded(fields, (("lon", 2),), rim_width, True)
    return padded(looped, (("lat", 1),), rim_width, False)


def local(
    adjoint_height,
    depth,
    wet,
    basis_lat,
    basis_lon,
    tile_owner,
    tile_patch,
    tile_count,
    prior_patches,
    prior_subfaults,
):
    highest = lax.Precision.HIGHEST
    lat_cells, lon_cells = adjoint_height.shape
    wet_depth = depth * wet.astype(jnp.float32)
    opening = widen(jnp.stack([adjoint_height, wet_depth]), 1)
    depth_rim = opening[1]
    blank = jnp.zeros_like(opening[0])
    height, east, north = adjoint_step(opening[0], blank, blank, depth_rim)
    for repeat in range(1, STEPS):
        widened = widen(jnp.stack([height, east, north]), 1)
        height, east, north = adjoint_step(widened[0], widened[1], widened[2], depth_rim)
    tile_rows = lat_cells // TS
    tile_cols = lon_cells // TS
    tile_total = tile_rows * tile_cols
    lon_devices = lax.axis_size("lon")
    capacity = max(2, 7 * tile_total // (4 * lon_devices))
    slot_total = capacity * lon_devices
    lat_basis = basis_lat.reshape(SUB, tile_rows, TS)
    partial_value = jnp.einsum(
        "sja,jac->sjc", lat_basis, height.reshape(tile_rows, TS, lon_cells), precision=highest
    )
    product = partial_value * basis_lon[:, None, :]
    sensitivity = jnp.sum(product.reshape(SUB, tile_rows, tile_cols, TS), axis=3).reshape(
        SUB, tile_total
    )
    active = (jnp.arange(SUB)[:, None] < tile_count.reshape(1, tile_total)).astype(jnp.float32)
    sensitivity = sensitivity * active
    owners = tile_owner.reshape(tile_total)
    patches = tile_patch.reshape(tile_total)
    owner_hot = (owners[:, None] == jnp.arange(lon_devices)[None, :]).astype(jnp.float32)
    earlier = (jnp.arange(tile_total)[:, None] > jnp.arange(tile_total)[None, :]).astype(
        jnp.float32
    )
    before = jnp.dot(earlier, owner_hot, precision=highest)
    rank_within = jnp.sum(before * owner_hot, axis=1).astype(jnp.int32)
    slot_index = owners * capacity + rank_within
    placing_mask = slot_index[:, None] == jnp.arange(slot_total)[None, :]
    placing = placing_mask.astype(jnp.float32)
    sent_values = jnp.dot(sensitivity, placing, precision=highest)
    sent_patches = jnp.sum(jnp.where(placing_mask, patches[:, None], 0), axis=0).reshape(
        1, slot_total
    )
    received, received_patches = (
        lax.all_to_all(sent_values, "lon", split_axis=1, concat_axis=1, tiled=True),
        lax.all_to_all(sent_patches, "lon", split_axis=1, concat_axis=1, tiled=True),
    )
    member = (received_patches.reshape(slot_total)[:, None] == jnp.arange(NPATCH)[None, :]).astype(
        jnp.float32
    )
    gathered = jnp.dot(received, member, precision=highest)
    covariance = prior_patches.reshape(NPATCH, NPATCH)
    mixed = jnp.einsum("sn,mn->sm", gathered, covariance, precision=highest)
    smoothed = jnp.einsum("st,sm->tm", prior_subfaults, mixed, precision=highest)
    replies = jnp.einsum("tm,km->tk", smoothed, member, precision=highest)
    returned = lax.all_to_all(replies, "lon", split_axis=1, concat_axis=1, tiled=True)
    tile_value = jnp.einsum("sk,tk->st", returned, placing, precision=highest) * active
    spread_value = tile_value.reshape(SUB, tile_rows, tile_cols, 1) * basis_lon.reshape(
        SUB, 1, tile_cols, TS
    )
    weighted = spread_value.reshape(SUB, tile_rows, lon_cells)
    gradient = jnp.einsum("sja,sjc->jac", lat_basis, weighted, precision=highest).reshape(
        lat_cells, lon_cells
    )
    return (height, gradient)


def solution(mesh):
    return jax.shard_map(
        local,
        mesh=mesh,
        in_specs=(
            P("lat", "lon"),
            P("lat", "lon"),
            P("lat", "lon"),
            P(None, "lat"),
            P(None, "lon"),
            P("lat", "lon"),
            P("lat", "lon"),
            P("lat", "lon"),
            P("lat", "lon", None, None),
            P(),
        ),
        out_specs=(P("lat", "lon"), P("lat", "lon")),
        check_vma=False,
    )
```

profile of v0, /device:TPU:7, one launch (start us, length us, event | category | flops | bytes accessed | tf_op | source)
XLA Modules:
  0.0 229.9 jit_solution(6770225124540143873)
XLA Ops:
  0.7 1.1 multiply_bitcast_fusion
  1.8 1.2 slice_maximum_fusion
  3.0 2.6 %collective-permute-start.1 = (f32[2,512,1]{2,1,0:T(8,128)S(1)}, f32[2,512,1]{2,1,0:T(8,128)S(1)}, u32[]{:S(2)}, u32[]{:S(2)}) collective-permute-start(f32[2,512,1]{2,1,0:T(8,128)S(1)} %get-tuple-element.42), channel_id=1, source_target_pairs={{8,0},{16,8},{24,16},{32,24},{40,32},{48,40},{56,48},{64,56},{72,6... | collective-permute-start | bytes 12296 | tf_op jit(solution)/shard_map/ppermute | solution.py:25
  5.6 3.1 %collective-permute-start = (f32[2,512,1]{2,1,0:T(8,128)S(1)}, f32[2,512,1]{2,1,0:T(8,128)S(1)}, u32[]{:S(2)}, u32[]{:S(2)}) collective-permute-start(f32[2,512,1]{2,1,0:T(8,128)S(1)} %get-tuple-element.41), channel_id=1, source_target_pairs={{0,8},{8,16},{16,24},{24,32},{32,40},{40,48},{48,56},{56,64},{64,7... | collective-permute-start | bytes 12296 | tf_op jit(solution)/shard_map/ppermute | solution.py:22
  8.7 4.9 %collective-permute-done.1 = f32[2,512,1]{2,1,0:T(8,128)S(1)} collective-permute-done((f32[2,512,1]{2,1,0:T(8,128)S(1)}, f32[2,512,1]{2,1,0:T(8,128)S(1)}, u32[]{:S(2)}, u32[]{:S(2)}) %collective-permute-start.1) | collective-permute-done | bytes 4128 | tf_op jit(solution)/shard_map/ppermute | solution.py:25
  13.6 14.1 %collective-permute-done = f32[2,512,1]{2,1,0:T(8,128)S(1)} collective-permute-done((f32[2,512,1]{2,1,0:T(8,128)S(1)}, f32[2,512,1]{2,1,0:T(8,128)S(1)}, u32[]{:S(2)}, u32[]{:S(2)}) %collective-permute-start) | collective-permute-done | bytes 4128 | tf_op jit(solution)/shard_map/ppermute | solution.py:22
  27.8 2.5 %collective-permute-start.3 = (f32[2,1,130]{2,1,0:T(1,128)S(1)}, f32[2,1,130]{2,1,0:T(1,128)S(1)}, u32[]{:S(2)}, u32[]{:S(2)}) collective-permute-start(f32[2,1,130]{2,1,0:T(1,128)S(1)} %get-tuple-element.22), channel_id=1, source_target_pairs={{1,0},{2,1},{3,2},{4,3},{5,4},{6,5},{7,6},{9,8},{10,9},{11,10},{12... | collective-permute-start | bytes 3128 | tf_op jit(solution)/shard_map/ppermute | solution.py:25
  30.2 8.8 %collective-permute-start.2 = (f32[2,1,130]{2,1,0:T(1,128)S(1)}, f32[2,1,130]{2,1,0:T(1,128)S(1)}, u32[]{:S(2)}, u32[]{:S(2)}) collective-permute-start(f32[2,1,130]{2,1,0:T(1,128)S(1)} %get-tuple-element.23), channel_id=1, source_target_pairs={{0,1},{1,2},{2,3},{3,4},{4,5},{5,6},{6,7},{8,9},{9,10},{10,11},{11... | collective-permute-start | bytes 3128 | tf_op jit(solution)/shard_map/ppermute | solution.py:22
  39.1 0.7 collective-permute-done.2
  39.8 0.5 pad_maximum_fusion
  40.4 0.9 pad_maximum_fusion.1
  41.4 0.4 fusion.26
  42.5 0.4 copy-done.5
  43.1 14.2 %collective-permute-start.5 = (f32[3,512,1]{1,2,0:T(1,128)S(1)}, f32[3,512,1]{1,2,0:T(1,128)S(1)}, u32[]{:S(2)}, u32[]{:S(2)}) collective-permute-start(f32[3,512,1]{1,2,0:T(1,128)S(1)} %copy.70), channel_id=1, source_target_pairs={{8,0},{16,8},{24,16},{32,24},{40,32},{48,40},{56,48},{64,56},{72,6... | collective-permute-start | bytes 18440 | tf_op jit(solution)/shard_map/ppermute | solution.py:25
  57.6 1.9 collective-permute-start.4
  59.8 0.8 collective-permute-done.4
  61.0 0.8 pad_maximum_fusion.64
  61.8 9.9 %collective-permute-start.6 = (f32[3,1,130]{2,1,0:T(1,128)S(1)}, f32[3,1,130]{2,1,0:T(1,128)S(1)}, u32[]{:S(2)}, u32[]{:S(2)}) collective-permute-start(f32[3,1,130]{2,1,0:T(1,128)S(1)} %get-tuple-element.19), channel_id=1, source_target_pairs={{0,1},{1,2},{2,3},{3,4},{4,5},{5,6},{6,7},{8,9},{9,10},{10,11},{11... | collective-permute-start | bytes 4688 | tf_op jit(solution)/shard_map/ppermute | solution.py:22
  71.7 1.9 collective-permute-start.7
  73.8 8.2 %collective-permute-done.7 = f32[3,1,130]{2,1,0:T(1,128)S(1)} collective-permute-done((f32[3,1,130]{2,1,0:T(1,128)S(1)}, f32[3,1,130]{2,1,0:T(1,128)S(1)}, u32[]{:S(2)}, u32[]{:S(2)}) %collective-permute-start.7) | collective-permute-done | bytes 1592 | tf_op jit(solution)/shard_map/ppermute | solution.py:25
  82.0 0.5 fusion.22
  82.8 0.7 copy-done.6
  83.5 0.7 fusion.19
  84.9 0.4 copy-done.3
  85.5 9.1 %collective-permute-start.9 = (f32[3,512,1]{1,2,0:T(1,128)S(1)}, f32[3,512,1]{1,2,0:T(1,128)S(1)}, u32[]{:S(2)}, u32[]{:S(2)}) collective-permute-start(f32[3,512,1]{1,2,0:T(1,128)S(1)} %copy.74), channel_id=1, source_target_pairs={{8,0},{16,8},{24,16},{32,24},{40,32},{48,40},{56,48},{64,56},{72,6... | collective-permute-start | bytes 18440 | tf_op jit(solution)/shard_map/ppermute | solution.py:25
  94.9 1.9 collective-permute-start.8
  97.4 0.6 collective-permute-done.8
  98.3 0.8 pad_maximum_fusion.59
  99.1 1.9 collective-permute-start.10
  101.0 3.4 %collective-permute-start.11 = (f32[3,1,130]{2,1,0:T(1,128)S(1)}, f32[3,1,130]{2,1,0:T(1,128)S(1)}, u32[]{:S(2)}, u32[]{:S(2)}) collective-permute-start(f32[3,1,130]{2,1,0:T(1,128)S(1)} %get-tuple-element.16), channel_id=1, source_target_pairs={{1,0},{2,1},{3,2},{4,3},{5,4},{6,5},{7,6},{9,8},{10,9},{11,10},{12... | collective-permute-start | bytes 4688 | tf_op jit(solution)/shard_map/ppermute | solution.py:25
  104.6 6.8 %collective-permute-done.11 = f32[3,1,130]{2,1,0:T(1,128)S(1)} collective-permute-done((f32[3,1,130]{2,1,0:T(1,128)S(1)}, f32[3,1,130]{2,1,0:T(1,128)S(1)}, u32[]{:S(2)}, u32[]{:S(2)}) %collective-permute-start.11) | collective-permute-done | bytes 1592 | tf_op jit(solution)/shard_map/ppermute | solution.py:25
  111.4 0.5 fusion.15
  112.1 0.7 copy-done.4
  112.8 0.7 fusion.12
  114.8 8.9 %collective-permute-start.13 = (f32[3,512,1]{1,2,0:T(1,128)S(1)}, f32[3,512,1]{1,2,0:T(1,128)S(1)}, u32[]{:S(2)}, u32[]{:S(2)}) collective-permute-start(f32[3,512,1]{1,2,0:T(1,128)S(1)} %copy.78), channel_id=1, source_target_pairs={{8,0},{16,8},{24,16},{32,24},{40,32},{48,40},{56,48},{64,56},{72,6... | collective-permute-start | bytes 18440 | tf_op jit(solution)/shard_map/ppermute | solution.py:25
  123.9 1.9 collective-permute-start.12
  126.0 0.8 all_to_all.22
  126.9 9.4 %all-to-all-start.1 = ((s32[1,128,3]{2,0,1:T(1,128)}), s32[1,128,3]{2,0,1:T(1,128)S(1)}, u32[]{:S(2)}, u32[]{:S(2)}) async-start(s32[1,128,3]{2,0,1:T(1,128)} %bitcast.29), calls=%async_computation.1 | async-start | bytes 131072 | tf_op jit(solution)/shard_map/all_to_all | solution.py:105
  136.9 1.4 pad_maximum_fusion.54
  138.3 2.1 collective-permute-start.14
  140.4 3.2 %collective-permute-start.15 = (f32[3,1,130]{2,1,0:T(1,128)}, f32[3,1,130]{2,1,0:T(1,128)}, u32[]{:S(2)}, u32[]{:S(2)}) collective-permute-start(f32[3,1,130]{2,1,0:T(1,128)} %get-tuple-element.14), channel_id=1, source_target_pairs={{1,0},{2,1},{3,2},{4,3},{5,4},{6,5},{7,6},{9,8},{10,9},{11,10},{12... | collective-permute-start | bytes 4688 | tf_op jit(solution)/shard_map/ppermute | solution.py:25
  143.6 0.6 multiply_add_fusion
  144.2 0.8 copy.82
  145.0 0.8 copy.81
  145.9 5.2 %collective-permute-done.15 = f32[3,1,130]{2,1,0:T(1,128)} collective-permute-done((f32[3,1,130]{2,1,0:T(1,128)}, f32[3,1,130]{2,1,0:T(1,128)}, u32[]{:S(2)}, u32[]{:S(2)}) %collective-permute-start.15) | collective-permute-done | bytes 1592 | tf_op jit(solution)/shard_map/ppermute | solution.py:25
  151.1 1.1 fusion.8
  152.5 0.7 copy-done.2
  153.2 1.4 fusion.5
  154.9 0.7 copy-done.9
  155.6 1.0 fusion
  156.7 0.6 copy.83
  157.4 0.5 bitcast_reduce_fusion
  158.1 0.4 fusion.32
  158.5 0.8 copy.87
  159.3 17.6 %all-to-all-start = ((f32[32,128,3]{0,2,1:T(4,128)}), f32[32,128,3]{0,2,1:T(4,128)S(1)}, u32[]{:S(2)}, u32[]{:S(2)}) async-start(f32[32,128,3]{0,2,1:T(4,128)} %copy.87), calls=%async_computation | async-start | bytes 524288 | tf_op jit(solution)/shard_map/all_to_all | solution.py:104
  176.9 0.5 broadcast.82
  177.4 0.8 reduce.3
  178.4 18.7 %all-to-all-done = f32[32,128,3]{0,2,1:T(4,128)S(1)} async-done(((f32[32,128,3]{0,2,1:T(4,128)}), f32[32,128,3]{0,2,1:T(4,128)S(1)}, u32[]{:S(2)}, u32[]{:S(2)}) %all-to-all-start) | async-done | bytes 49184 | tf_op jit(solution)/shard_map/all_to_all | solution.py:104
  197.1 0.4 fusion.31
  198.1 0.4 fusion.30
  198.6 28.4 %all_to_all.30 = f32[32,128,3]{0,2,1:T(4,128)S(1)} all-to-all(f32[32,128,3]{0,2,1:T(4,128)S(1)} %all_to_all.24), channel_id=1, replica_groups=mesh['lon'=128,'lat'=8] {'lon'}, dimensions={1} | all-to-all | bytes 98304 | tf_op jit(solution)/shard_map/all_to_all | solution.py:115
  227.1 0.4 convolution_select_fusion.1
  227.9 0.7 copy.93
  228.6 1.3 fusion.28
  (86 shorter events, 9.5 us)
Async XLA Ops:
  0.6 196.9 %copy-start = (f32[1,1,256,256]{3,2,1,0:T(8,128)S(1)}, f32[1,1,256,256]{3,2,1,0:T(8,128)}, u32[]{:S(2)}) copy-start(f32[1,1,256,256]{3,2,1,0:T(8,128)} %param.18) | copy-start | bytes 786436
  0.6 27.1 %copy-start.7 = (f32[512,128]{1,0:T(8,128)S(1)}, f32[512,128]{1,0:T(8,128)}, u32[]{:S(2)}) copy-start(f32[512,128]{1,0:T(8,128)} %param.10) | copy-start | bytes 786436
  3.0 10.6 %collective-permute-start.1 = (f32[2,512,1]{2,1,0:T(8,128)S(1)}, f32[2,512,1]{2,1,0:T(8,128)S(1)}, u32[]{:S(2)}, u32[]{:S(2)}) collective-permute-start(f32[2,512,1]{2,1,0:T(8,128)S(1)} %get-tuple-element.42), channel_id=1, source_target_pairs={{8,0},{16,8},{24,16},{32,24},{40,32},{48,40},{56,48},{64,56},{72,6... | collective-permute-start | bytes 12296 | tf_op jit(solution)/shard_map/ppermute | solution.py:25
  5.6 22.1 %collective-permute-start = (f32[2,512,1]{2,1,0:T(8,128)S(1)}, f32[2,512,1]{2,1,0:T(8,128)S(1)}, u32[]{:S(2)}, u32[]{:S(2)}) collective-permute-start(f32[2,512,1]{2,1,0:T(8,128)S(1)} %get-tuple-element.41), channel_id=1, source_target_pairs={{0,8},{8,16},{16,24},{24,32},{32,40},{40,48},{48,56},{56,64},{64,7... | collective-permute-start | bytes 12296 | tf_op jit(solution)/shard_map/ppermute | solution.py:22
  27.8 11.3 %collective-permute-start.3 = (f32[2,1,130]{2,1,0:T(1,128)S(1)}, f32[2,1,130]{2,1,0:T(1,128)S(1)}, u32[]{:S(2)}, u32[]{:S(2)}) collective-permute-start(f32[2,1,130]{2,1,0:T(1,128)S(1)} %get-tuple-element.22), channel_id=1, source_target_pairs={{1,0},{2,1},{3,2},{4,3},{5,4},{6,5},{7,6},{9,8},{10,9},{11,10},{12... | collective-permute-start | bytes 3128 | tf_op jit(solution)/shard_map/ppermute | solution.py:25
  30.2 9.6 %collective-permute-start.2 = (f32[2,1,130]{2,1,0:T(1,128)S(1)}, f32[2,1,130]{2,1,0:T(1,128)S(1)}, u32[]{:S(2)}, u32[]{:S(2)}) collective-permute-start(f32[2,1,130]{2,1,0:T(1,128)S(1)} %get-tuple-element.23), channel_id=1, source_target_pairs={{0,1},{1,2},{2,3},{3,4},{4,5},{5,6},{6,7},{8,9},{9,10},{10,11},{11... | collective-permute-start | bytes 3128 | tf_op jit(solution)/shard_map/ppermute | solution.py:22
  42.1 0.7 copy-start.5
  43.1 16.4 %collective-permute-start.5 = (f32[3,512,1]{1,2,0:T(1,128)S(1)}, f32[3,512,1]{1,2,0:T(1,128)S(1)}, u32[]{:S(2)}, u32[]{:S(2)}) collective-permute-start(f32[3,512,1]{1,2,0:T(1,128)S(1)} %copy.70), channel_id=1, source_target_pairs={{8,0},{16,8},{24,16},{32,24},{40,32},{48,40},{56,48},{64,56},{72,6... | collective-permute-start | bytes 18440 | tf_op jit(solution)/shard_map/ppermute | solution.py:25
  57.6 3.1 %collective-permute-start.4 = (f32[3,512,1]{1,2,0:T(1,128)S(1)}, f32[3,512,1]{1,2,0:T(1,128)S(1)}, u32[]{:S(2)}, u32[]{:S(2)}) collective-permute-start(f32[3,512,1]{1,2,0:T(1,128)S(1)} %copy.69), channel_id=1, source_target_pairs={{0,8},{8,16},{16,24},{24,32},{32,40},{40,48},{48,56},{56,64},{64,7... | collective-permute-start | bytes 18440 | tf_op jit(solution)/shard_map/ppermute | solution.py:22
  60.9 12.7 %copy-start.15 = (s32[32,8]{0,1:T(8,128)S(1)}, s32[32,8]{0,1:T(8,128)}, u32[]{:S(2)}) copy-start(s32[32,8]{0,1:T(8,128)} %param.15) | copy-start | bytes 3076
  61.8 12.0 %collective-permute-start.6 = (f32[3,1,130]{2,1,0:T(1,128)S(1)}, f32[3,1,130]{2,1,0:T(1,128)S(1)}, u32[]{:S(2)}, u32[]{:S(2)}) collective-permute-start(f32[3,1,130]{2,1,0:T(1,128)S(1)} %get-tuple-element.19), channel_id=1, source_target_pairs={{0,1},{1,2},{2,3},{3,4},{4,5},{5,6},{6,7},{8,9},{9,10},{10,11},{11... | collective-permute-start | bytes 4688 | tf_op jit(solution)/shard_map/ppermute | solution.py:22
  71.7 10.4 %collective-permute-start.7 = (f32[3,1,130]{2,1,0:T(1,128)S(1)}, f32[3,1,130]{2,1,0:T(1,128)S(1)}, u32[]{:S(2)}, u32[]{:S(2)}) collective-permute-start(f32[3,1,130]{2,1,0:T(1,128)S(1)} %get-tuple-element.18), channel_id=1, source_target_pairs={{1,0},{2,1},{3,2},{4,3},{5,4},{6,5},{7,6},{9,8},{10,9},{11,10},{12... | collective-permute-start | bytes 4688 | tf_op jit(solution)/shard_map/ppermute | solution.py:25
  82.5 1.0 copy-start.6
  84.5 0.7 copy-start.3
  85.5 11.6 %collective-permute-start.9 = (f32[3,512,1]{1,2,0:T(1,128)S(1)}, f32[3,512,1]{1,2,0:T(1,128)S(1)}, u32[]{:S(2)}, u32[]{:S(2)}) collective-permute-start(f32[3,512,1]{1,2,0:T(1,128)S(1)} %copy.74), channel_id=1, source_target_pairs={{8,0},{16,8},{24,16},{32,24},{40,32},{48,40},{56,48},{64,56},{72,6... | collective-permute-start | bytes 18440 | tf_op jit(solution)/shard_map/ppermute | solution.py:25
  94.9 3.1 %collective-permute-start.8 = (f32[3,512,1]{1,2,0:T(1,128)S(1)}, f32[3,512,1]{1,2,0:T(1,128)S(1)}, u32[]{:S(2)}, u32[]{:S(2)}) collective-permute-start(f32[3,512,1]{1,2,0:T(1,128)S(1)} %copy.73), channel_id=1, source_target_pairs={{0,8},{8,16},{16,24},{24,32},{32,40},{40,48},{48,56},{56,64},{64,7... | collective-permute-start | bytes 18440 | tf_op jit(solution)/shard_map/ppermute | solution.py:22
  98.3 6.1 %copy-start.16 = (s32[32,8]{0,1:T(8,128)S(1)}, s32[32,8]{0,1:T(8,128)}, u32[]{:S(2)}) copy-start(s32[32,8]{0,1:T(8,128)} %param.16) | copy-start | bytes 3076
  99.1 5.5 %collective-permute-start.10 = (f32[3,1,130]{2,1,0:T(1,128)S(1)}, f32[3,1,130]{2,1,0:T(1,128)S(1)}, u32[]{:S(2)}, u32[]{:S(2)}) collective-permute-start(f32[3,1,130]{2,1,0:T(1,128)S(1)} %get-tuple-element.17), channel_id=1, source_target_pairs={{0,1},{1,2},{2,3},{3,4},{4,5},{5,6},{6,7},{8,9},{9,10},{10,11},{11... | collective-permute-start | bytes 4688 | tf_op jit(solution)/shard_map/ppermute | solution.py:22
  101.0 10.4 %collective-permute-start.11 = (f32[3,1,130]{2,1,0:T(1,128)S(1)}, f32[3,1,130]{2,1,0:T(1,128)S(1)}, u32[]{:S(2)}, u32[]{:S(2)}) collective-permute-start(f32[3,1,130]{2,1,0:T(1,128)S(1)} %get-tuple-element.16), channel_id=1, source_target_pairs={{1,0},{2,1},{3,2},{4,3},{5,4},{6,5},{7,6},{9,8},{10,9},{11,10},{12... | collective-permute-start | bytes 4688 | tf_op jit(solution)/shard_map/ppermute | solution.py:25
  104.4 21.5 %copy-start.13 = (s32[256]{0:T(256)}, s32[256]{0:T(256)S(1)}, u32[]{:S(2)}) copy-start(s32[256]{0:T(256)S(1)} %convert_add_fusion) | copy-start | bytes 3076
  111.9 1.0 copy-start.4
  113.9 0.7 copy-start.1
  114.8 21.4 %collective-permute-start.13 = (f32[3,512,1]{1,2,0:T(1,128)S(1)}, f32[3,512,1]{1,2,0:T(1,128)S(1)}, u32[]{:S(2)}, u32[]{:S(2)}) collective-permute-start(f32[3,512,1]{1,2,0:T(1,128)S(1)} %copy.78), channel_id=1, source_target_pairs={{8,0},{16,8},{24,16},{32,24},{40,32},{48,40},{56,48},{64,56},{72,6... | collective-permute-start | bytes 18440 | tf_op jit(solution)/shard_map/ppermute | solution.py:25
  123.9 12.6 %collective-permute-start.12 = (f32[3,512,1]{1,2,0:T(1,128)S(1)}, f32[3,512,1]{1,2,0:T(1,128)S(1)}, u32[]{:S(2)}, u32[]{:S(2)}) collective-permute-start(f32[3,512,1]{1,2,0:T(1,128)S(1)} %copy.77), channel_id=1, source_target_pairs={{0,8},{8,16},{16,24},{24,32},{32,40},{40,48},{48,56},{56,64},{64,7... | collective-permute-start | bytes 18440 | tf_op jit(solution)/shard_map/ppermute | solution.py:22
  126.9 32.4 %all-to-all-start.1 = ((s32[1,128,3]{2,0,1:T(1,128)}), s32[1,128,3]{2,0,1:T(1,128)S(1)}, u32[]{:S(2)}, u32[]{:S(2)}) async-start(s32[1,128,3]{2,0,1:T(1,128)} %bitcast.29), calls=%async_computation.1 | async-start | bytes 131072 | tf_op jit(solution)/shard_map/all_to_all | solution.py:105
  136.9 7.3 %copy-start.11 = (f32[32,512]{1,0:T(8,128)S(1)}, f32[32,512]{1,0:T(8,128)}, u32[]{:S(2)}) copy-start(f32[32,512]{1,0:T(8,128)} %param.13) | copy-start | bytes 196612
  138.3 7.6 %collective-permute-start.14 = (f32[3,1,130]{2,1,0:T(1,128)}, f32[3,1,130]{2,1,0:T(1,128)}, u32[]{:S(2)}, u32[]{:S(2)}) collective-permute-start(f32[3,1,130]{2,1,0:T(1,128)} %get-tuple-element.15), channel_id=1, source_target_pairs={{0,1},{1,2},{2,3},{3,4},{4,5},{5,6},{6,7},{8,9},{9,10},{10,11},{11... | collective-permute-start | bytes 4688 | tf_op jit(solution)/shard_map/ppermute | solution.py:22
  140.4 10.7 %collective-permute-start.15 = (f32[3,1,130]{2,1,0:T(1,128)}, f32[3,1,130]{2,1,0:T(1,128)}, u32[]{:S(2)}, u32[]{:S(2)}) collective-permute-start(f32[3,1,130]{2,1,0:T(1,128)} %get-tuple-element.14), channel_id=1, source_target_pairs={{1,0},{2,1},{3,2},{4,3},{5,4},{6,5},{7,6},{9,8},{10,9},{11,10},{12... | collective-permute-start | bytes 4688 | tf_op jit(solution)/shard_map/ppermute | solution.py:25
  152.2 1.0 copy-start.2
  154.6 1.1 copy-start.8
  154.6 1.1 copy-start.10
  154.9 0.7 copy-start.9
  157.3 0.7 copy-start.14
  157.3 0.7 copy-start.17
  158.1 39.8 %copy-start.12 = (f32[32,32]{1,0:T(8,128)S(1)}, f32[32,32]{1,0:T(8,128)}, u32[]{:S(2)}) copy-start(f32[32,32]{1,0:T(8,128)} %param.19) | copy-start | bytes 12292
  159.3 37.7 %all-to-all-start = ((f32[32,128,3]{0,2,1:T(4,128)}), f32[32,128,3]{0,2,1:T(4,128)S(1)}, u32[]{:S(2)}, u32[]{:S(2)}) async-start(f32[32,128,3]{0,2,1:T(4,128)} %copy.87), calls=%async_computation | async-start | bytes 524288 | tf_op jit(solution)/shard_map/all_to_all | solution.py:104
where the time goes:
time: 233 us; the launch traced here: 230 us
  starting transfers between devices  104 us (45%)
  waiting for transfers between devices  60 us (26%)
  blocking collectives  28.4 us (12%)
  other arithmetic  16.4 us (7%)
  local copies, waits for them, and re-layouts  14.8 us (6%)
  matrix products  4.64 us (2%)
    ppermute x8, starting transfers between devices, padded(): lax.ppermute(lax.slice_in_dim(block, 0, width, axis=dim), axis, backward)  45.7 us
    ppermute x8, starting transfers between devices, padded(): lax.ppermute(lax.slice_in_dim(block, block.shape[dim] - width, None, axis...  31.6 us
    all_to_all x1, blocking collectives, local(): lax.all_to_all(replies, 'lon', split_axis=1, concat_axis=1, tiled=True)  28.4 us
    ppermute x8, waiting for transfers between devices, padded(): lax.ppermute(lax.slice_in_dim(block, 0, width, axis=dim), axis, backward)  25.2 us
    all_to_all x1, waiting for transfers between devices, local(): lax.all_to_all(sent_values, 'lon', split_axis=1, concat_axis=1, tiled=True)  18.7 us
    all_to_all x1, starting transfers between devices, local(): lax.all_to_all(sent_values, 'lon', split_axis=1, concat_axis=1, tiled=True)  17.6 us
    ppermute x8, waiting for transfers between devices, padded(): lax.ppermute(lax.slice_in_dim(block, block.shape[dim] - width, None, axis...  16.2 us
    all_to_all x1, starting transfers between devices, local(): lax.all_to_all(sent_patches, 'lon', split_axis=1, concat_axis=1, tiled=True)  9.36 us
  transfers between devices with their start and end apart: 18, of which 9 were waited for; matrix products, arithmetic and copies ran while one was open for 6% of the time, Pallas kernels for 0%

commit v1 on v0

v1 whole, which is shorter than its diff:
```python
import jax
import jax.numpy as jnp
from jax import lax
from jax.experimental import pallas as pl
from jax.experimental.pallas import tpu as pltpu
from jax.sharding import PartitionSpec as P

STEPS = 4
RIM = 4
TS = 16
SUB = 32
NPATCH = 256
CAP = 3
COURANT = 0.6
LANES = 128
F32 = jnp.float32
BF16 = jnp.bfloat16


def iota(shape, dim):
    return lax.broadcasted_iota(jnp.int32, shape, dim)


def parts(x):
    high = x.astype(BF16)
    return high, (x - high.astype(F32)).astype(BF16)


def dot(a, b):
    return lax.dot_general(a, b, (((1,), (0,)), ((), ())), preferred_element_type=F32)


def dot_t(a, b):
    return lax.dot_general(a, b, (((1,), (1,)), ((), ())), preferred_element_type=F32)


def one_hot_dot(hot, x):
    high, low = parts(x)
    return dot(hot, high) + dot(hot, low)


def dot3(a, b, product=dot):
    a_high, a_low = parts(a)
    b_high, b_low = parts(b)
    return product(a_high, b_high) + (product(a_high, b_low) + product(a_low, b_high))


def spread_lon(basis_lon):
    tiles = LANES // TS
    tall = jnp.concatenate([basis_lon] * tiles, axis=0)
    inside = iota(tall.shape, 0) // SUB == iota(tall.shape, 1) // TS
    return jnp.where(inside, tall, 0.0)


def edge_columns(height, wet_depth):
    lane = iota(height.shape, 1)
    near = jnp.where(lane < RIM, height, pltpu.roll(wet_depth, RIM, 1))
    far = jnp.where(lane >= LANES - RIM, height, pltpu.roll(wet_depth, LANES - RIM, 1))
    return jnp.where(lane < LANES // 2, near, far)


def prepare(h_ref, d_ref, w_ref, lat_ref, owner_ref, patch_ref, count_ref,
            edge_ref, lat4_ref, hot_ref, hot_t_ref, mask_ref):
    height = h_ref[...]
    wet_depth = d_ref[...] * w_ref[...].astype(F32)
    edges = edge_columns(height, wet_depth).T
    edge_ref[0:8, :] = edges[0:8]
    edge_ref[8:16, :] = edges[LANES - 8:LANES]
    lat4_ref[...] = jnp.concatenate([lat_ref[...]] * 4, axis=0).T

    def column(ref):
        table = ref[...].astype(F32)
        flat = jnp.concatenate([table[:, k:k + 1] for k in range(table.shape[1])], axis=0)
        return jnp.broadcast_to(flat, (flat.shape[0], LANES))

    owner = column(owner_ref)
    patch = column(patch_ref)
    count = column(count_ref)
    owner_row = owner.T
    total = owner.shape[0]
    hot_t_ref[...] = (owner == iota(owner.shape, 1).astype(F32)).astype(BF16)
    hot_ref[...] = (owner_row == iota(owner_row.shape, 0).astype(F32)).astype(BF16)
    rank = jnp.zeros((total, LANES), F32)
    for q in range(total // LANES):
        row = jnp.broadcast_to(owner_row[0:1, q * LANES:(q + 1) * LANES], (total, LANES))
        earlier = iota((total, LANES), 1) + q * LANES < iota((total, LANES), 0)
        rank = rank + jnp.where(earlier & (row == owner), 1.0, 0.0)
    rank = jnp.broadcast_to(jnp.sum(rank, axis=1, keepdims=True), (total, LANES))
    lane = iota((total, LANES), 1)
    group = (lane // SUB).astype(F32)
    place = (lane % SUB).astype(F32)
    live = jnp.where((rank == group) & (place < count), 1.0, 0.0)
    number = jnp.where(rank == place, patch, 0.0)
    mask_ref[...] = jnp.where(lane < CAP * SUB, live, number)


def rims(parity_lat, ra, rb):
    south = jnp.where(parity_lat == 0, ra, rb)
    north = jnp.where(parity_lat == 0, rb, ra)
    return north, south


def corners(par_ref, edge_ref, ra_ref, rb_ref, first_ref, second_ref, east_ref, west_ref):
    north, south = rims(par_ref[1], ra_ref[...], rb_ref[...])
    row = iota((8, LANES), 0)
    top = edge_columns(south, pltpu.roll(south, 4, 0))
    low = edge_columns(pltpu.roll(north, 4, 0), north)
    block = jnp.concatenate(
        [jnp.where(row < 4, top, 0.0), jnp.zeros((LANES - 16, LANES), F32), jnp.where(row < 4, 0.0, low)],
        axis=0,
    ).T
    west = jnp.concatenate([edge_ref[0:8, :], block[0:8]], axis=1)
    east = jnp.concatenate([edge_ref[8:16, :], block[LANES - 8:LANES]], axis=1)
    west_ref[...] = west
    east_ref[...] = east
    first_ref[...] = jnp.where(par_ref[0] == 0, east, west)
    second_ref[...] = jnp.where(par_ref[0] == 0, west, east)


def flux_update(height, east, north, ce, cn, right, below):
    east = east + ce * (right - height)
    north = north + cn * (below - height)
    return east, north


def strip(height, wet_depth):
    rows, lanes = height.shape
    ce = COURANT * jnp.minimum(wet_depth, pltpu.roll(wet_depth, rows - 1, 0))
    cn = COURANT * jnp.minimum(wet_depth, pltpu.roll(wet_depth, lanes - 1, 1))
    east = jnp.zeros_like(height)
    north = jnp.zeros_like(height)
    heights, easts = [height], []
    for _ in range(STEPS):
        east, north = flux_update(
            height, east, north, ce, cn, pltpu.roll(height, rows - 1, 0), pltpu.roll(height, lanes - 1, 1)
        )
        height = (
            height
            + COURANT * (east - pltpu.roll(east, 1, 0))
            + COURANT * (north - pltpu.roll(north, 1, 1))
        )
        heights.append(height)
        easts.append(east)
    return heights, easts


def forward(par_ref, h_ref, d_ref, w_ref, na_ref, nb_ref, east_ref, west_ref, ea_ref, eb_ref,
            lon_ref, lat4_ref, hot_ref, mask_ref, out_ref, send_ref):
    rows_own = h_ref.shape[0]
    north_rim, south_rim = rims(par_ref[1], na_ref[...], nb_ref[...])
    from_east = jnp.where(par_ref[0] == 0, ea_ref[...], eb_ref[...])
    from_west = jnp.where(par_ref[0] == 0, eb_ref[...], ea_ref[...])
    own_west, own_east = west_ref[...], east_ref[...]
    west_h = jnp.concatenate([from_west[4:8], own_west[0:4]], axis=0)
    west_d = jnp.concatenate([from_west[0:4], own_west[4:8]], axis=0)
    east_h = jnp.concatenate([own_east[4:8], from_east[0:4]], axis=0)
    east_d = jnp.concatenate([own_east[0:4], from_east[4:8]], axis=0)
    _, west_easts = strip(west_h, west_d)
    east_heights, _ = strip(east_h, east_d)
    lines = [e[3:4] for e in west_easts] + [x[4:5] for x in east_heights[:STEPS]] + [east_d[4:5]]
    lines.append(jnp.zeros((LANES - len(lines), lines[0].shape[1]), F32))
    table = jnp.concatenate(lines, axis=0).T
    table = jnp.concatenate([table[rows_own + LANES - 8:], table[:rows_own + 8]], axis=0)

    row8 = iota((8, LANES), 0)
    height = jnp.concatenate(
        [
            jnp.where(row8 < 4, 0.0, pltpu.roll(north_rim, 4, 0)),
            h_ref[...],
            jnp.where(row8 < 4, south_rim, 0.0),
        ],
        axis=0,
    )
    wet_depth = jnp.concatenate(
        [
            jnp.where(row8 < 4, 0.0, north_rim),
            d_ref[...] * w_ref[...].astype(F32),
            jnp.where(row8 < 4, pltpu.roll(south_rim, 4, 0), 0.0),
        ],
        axis=0,
    )
    rows = height.shape[0]
    lane = iota(height.shape, 1)

    def line(index):
        return jnp.broadcast_to(table[:, index:index + 1], height.shape)

    def right_of(field, index):
        return jnp.where(lane == LANES - 1, line(index), pltpu.roll(field, LANES - 1, 1))

    ce = COURANT * jnp.minimum(wet_depth, right_of(wet_depth, 2 * STEPS))
    cn = COURANT * jnp.minimum(wet_depth, pltpu.roll(wet_depth, rows - 1, 0))
    east = jnp.zeros_like(height)
    north = jnp.zeros_like(height)
    for k in range(STEPS):
        east, north = flux_update(
            height, east, north, ce, cn, right_of(height, STEPS + k), pltpu.roll(height, rows - 1, 0)
        )
        before = jnp.where(lane == 0, line(k), pltpu.roll(east, 1, 1))
        height = height + COURANT * (east - before) + COURANT * (north - pltpu.roll(north, 1, 0))
    final = height[8:8 + rows_own]
    out_ref[...] = final

    product = dot3(final, spread_lon(lon_ref[...]), dot_t)
    lat4 = lat4_ref[...]
    product = product * jnp.concatenate([lat4, lat4], axis=1)
    tile_rows = rows_own // TS
    sums = jnp.sum(product.reshape(tile_rows, TS, product.shape[1]), axis=1)
    group = iota((tile_rows, LANES), 1) // SUB
    stacked = []
    for q in range(sums.shape[1] // LANES):
        for g in range(4):
            own = jnp.where(group == g, sums[:, q * LANES:(q + 1) * LANES], 0.0)
            own = own + pltpu.roll(own, 2 * SUB, 1)
            stacked.append(own + pltpu.roll(own, SUB, 1))
    values = jnp.concatenate(stacked, axis=0)
    mask = mask_ref[...]
    filled = jnp.where(iota(mask.shape, 1) < CAP * SUB, values * mask, mask)
    send_ref[...] = one_hot_dot(hot_ref[...], filled)


def smooth(recv_ref, prior_ref, sub_ref, reply_ref):
    received = recv_ref[...]
    turned = received.T
    devices = received.shape[0]
    group = iota((devices, LANES), 1) // SUB
    gathered = jnp.zeros((NPATCH, LANES), F32)
    for r in range(CAP):
        line = jnp.broadcast_to(turned[CAP * SUB + r:CAP * SUB + r + 1], (NPATCH, devices))
        member = (line == iota((NPATCH, devices), 0).astype(F32)).astype(BF16)
        gathered = gathered + one_hot_dot(member, jnp.where(group == r, received, 0.0))
    mixed = dot3(prior_ref[...], gathered)
    sub = jnp.concatenate([sub_ref[...]] * 4, axis=1)
    sub = jnp.concatenate([sub] * CAP + [jnp.zeros_like(sub)], axis=0)
    smoothed = dot3(mixed, sub)
    group = iota(smoothed.shape, 1) // SUB
    reply = jnp.zeros((devices, LANES), F32)
    for r in range(CAP):
        line = jnp.broadcast_to(received[:, CAP * SUB + r:CAP * SUB + r + 1], (devices, NPATCH))
        member = (line == iota((devices, NPATCH), 1).astype(F32)).astype(BF16)
        reply = reply + one_hot_dot(member, jnp.where(group == r, smoothed, 0.0))
    reply_ref[...] = reply


def backward(ret_ref, hot_t_ref, mask_ref, lat4_ref, lon_ref, out_ref):
    mask = mask_ref[...]
    picked = one_hot_dot(hot_t_ref[...], ret_ref[...])
    picked = jnp.where(iota(mask.shape, 1) < CAP * SUB, picked * mask, 0.0)
    picked = picked + pltpu.roll(picked, 2 * SUB, 1)
    picked = picked + pltpu.roll(picked, SUB, 1)
    tile_rows = out_ref.shape[0] // TS
    group = iota((tile_rows, LANES), 1) // SUB
    halves = []
    for q in range(2):
        half = picked[4 * q * tile_rows:(4 * q + 1) * tile_rows]
        for g in range(1, 4):
            block = picked[(4 * q + g) * tile_rows:(4 * q + g + 1) * tile_rows]
            half = jnp.where(group == g, block, half)
        halves.append(half)
    value = jnp.concatenate(halves, axis=1)
    wide = jnp.broadcast_to(value[:, None, :], (tile_rows, TS, value.shape[1])).reshape(
        out_ref.shape[0], value.shape[1]
    )
    lat4 = lat4_ref[...]
    weighted = wide * jnp.concatenate([lat4, lat4], axis=1)
    out_ref[...] = dot3(weighted, spread_lon(lon_ref[...]))


VMEM = pl.BlockSpec(memory_space=pltpu.VMEM)
SMEM = pl.BlockSpec(memory_space=pltpu.SMEM)


def call(kernel, outs, *args, scalars=0):
    return pl.pallas_call(
        kernel,
        out_shape=[jax.ShapeDtypeStruct(shape, dtype) for shape, dtype in outs],
        in_specs=[SMEM] * scalars + [VMEM] * (len(args) - scalars),
        out_specs=[VMEM] * len(outs),
        compiler_params=pltpu.CompilerParams(vmem_limit_bytes=32 * 1024 * 1024),
    )(*args)


def swap_pairs(axis, first, periodic):
    count = lax.axis_size(axis)
    pairs = []
    for a in range(first, count, 2):
        b = a + 1
        if b == count:
            if not periodic:
                continue
            b = 0
        pairs += [(a, b), (b, a)]
    return pairs


def swap(payload, axis, periodic):
    return [
        lax.ppermute(x, axis, swap_pairs(axis, first, periodic)) for first, x in enumerate(payload)
    ]


def local(
    adjoint_height,
    depth,
    wet,
    basis_lat,
    basis_lon,
    tile_owner,
    tile_patch,
    tile_count,
    prior_patches,
    prior_subfaults,
):
    rows, cols = adjoint_height.shape
    lon_devices = lax.axis_size("lon")
    total = (rows // TS) * (cols // TS)
    parity = jnp.stack([lax.axis_index("lon") % 2, lax.axis_index("lat") % 2]).astype(jnp.int32)

    def edge_rows(start):
        def cut(x):
            return lax.dynamic_slice_in_dim(x, start, RIM, axis=0)
        return jnp.concatenate([cut(adjoint_height), cut(depth) * cut(wet).astype(F32)], axis=0)

    last = rows - RIM
    a_rows = edge_rows(jnp.where(parity[1] == 0, last, 0))
    b_rows = edge_rows(jnp.where(parity[1] == 0, 0, last))
    north_a, north_b = swap([a_rows, b_rows], "lat", False)
    edges, lat4, hot, hot_t, mask = call(
        prepare,
        [
            ((16, rows), F32),
            ((rows, LANES), F32),
            ((lon_devices, total), BF16),
            ((total, lon_devices), BF16),
            ((total, LANES), F32),
        ],
        adjoint_height, depth, wet, basis_lat, tile_owner, tile_patch, tile_count,
    )
    wide = ((8, rows + LANES), F32)
    first, second, east, west = call(
        corners, [wide] * 4, parity, edges, north_a, north_b, scalars=1
    )
    east_a, east_b = swap([first, second], "lon", True)
    final, sent = call(
        forward,
        [((rows, cols), F32), ((lon_devices, LANES), F32)],
        parity, adjoint_height, depth, wet, north_a, north_b, east, west, east_a, east_b,
        basis_lon, lat4, hot, mask,
        scalars=1,
    )
    received = lax.all_to_all(sent, "lon", split_axis=0, concat_axis=0, tiled=True)
    (replies,) = call(
        smooth,
        [((lon_devices, LANES), F32)],
        received, prior_patches.reshape(NPATCH, NPATCH), prior_subfaults,
    )
    returned = lax.all_to_all(replies, "lon", split_axis=0, concat_axis=0, tiled=True)
    (gradient,) = call(
        backward, [((rows, cols), F32)], returned, hot_t, mask, lat4, basis_lon
    )
    return (final, gradient)


def solution(mesh):
    return jax.shard_map(
        local,
        mesh=mesh,
        in_specs=(
            P("lat", "lon"),
            P("lat", "lon"),
            P("lat", "lon"),
            P(None, "lat"),
            P(None, "lon"),
            P("lat", "lon"),
            P("lat", "lon"),
            P("lat", "lon"),
            P("lat", "lon", None, None),
            P(),
        ),
        out_specs=(P("lat", "lon"), P("lat", "lon")),
        check_vma=False,
    )
```

time: 233 us -> 93.1 us (0.40); the launches traced: 230 us -> 92.6 us
  starting transfers between devices: 104 us -> 15.8 us
  waiting for transfers between devices: 60 us -> 2.89 us
  blocking collectives: 28.4 us -> 59.3 us
  other arithmetic: 16.4 us -> 0.91 us
  local copies, waits for them, and re-layouts: 14.8 us -> 4.92 us
  Pallas kernels: 0 us -> 7.96 us
  matrix products: 4.64 us -> 0 us
    ppermute x16 -> x4, starting transfers between devices: 77.4 us -> 15.8 us  [swap(): lax.ppermute(x, axis, swap_pairs(axis, first, periodic))]
    ppermute x16 -> x4, waiting for transfers between devices: 41.4 us -> 2.89 us  [swap(): lax.ppermute(x, axis, swap_pairs(axis, first, periodic))]
    all_to_all x1 -> x2, blocking collectives: 28.4 us -> 59.3 us  [the longest x1 39.3 us: local(): lax.all_to_all(sent, 'lon', split_axis=0, concat_axis=0, tiled=True)]
    all_to_all x2 -> x0, starting transfers between devices: 26.9 us -> none  [the longest x1 17.6 us: local(): lax.all_to_all(sent_values, 'lon', split_axis=1, concat_axis=1, tiled=True)]
    all_to_all x2 -> x0, waiting for transfers between devices: 18.7 us -> none  [the longest x1 18.7 us: local(): lax.all_to_all(sent_values, 'lon', split_axis=1, concat_axis=1, tiled=True)]
    pallas_call x0 -> x5, Pallas kernels: none -> 7.96 us  [call(): pl.pallas_call(kernel, out_shape=[jax.ShapeDtypeStruct(shape, dtype) for...]
    dot_general x9 -> x0, matrix products: 4.64 us -> none  [the longest x1 1.31 us: local(): jnp.einsum('sja,sjc->jac', lat_basis, weighted, precision=highest)]
    concatenate x6 -> x2, other arithmetic: 4.45 us -> 0.02 us  [edge_rows(): jnp.concatenate([cut(adjoint_height), cut(depth) * cut(wet).astype(F32)],...]
  transfers between devices with their start and end apart: 18 -> 4, of which waited for: 9 -> 1; matrix products, arithmetic and copies ran while one was open for 6% -> 0% of each run, Pallas kernels for 0% -> 1%
where the time goes in v1:
time: 93.1 us; the launch traced here: 92.6 us
  blocking collectives  59.3 us (64%)
  starting transfers between devices  15.8 us (17%)
  Pallas kernels  7.96 us (9%)
  local copies, waits for them, and re-layouts  4.92 us (5%)
  waiting for transfers between devices  2.89 us (3%)
    all_to_all x1, blocking collectives, local(): lax.all_to_all(sent, 'lon', split_axis=0, concat_axis=0, tiled=True)  39.3 us
    all_to_all x1, blocking collectives, local(): lax.all_to_all(replies, 'lon', split_axis=0, concat_axis=0, tiled=True)  20 us
    ppermute x4, starting transfers between devices, swap(): lax.ppermute(x, axis, swap_pairs(axis, first, periodic))  15.8 us
    pallas_call x5, Pallas kernels, call(): pl.pallas_call(kernel, out_shape=[jax.ShapeDtypeStruct(shape, dtype) for...  7.96 us
    unnamed x25, local copies, waits for them, and re-layouts  4.92 us
    ppermute x4, waiting for transfers between devices, swap(): lax.ppermute(x, axis, swap_pairs(axis, first, periodic))  2.89 us
  transfers between devices with their start and end apart: 4, of which 1 were waited for; matrix products, arithmetic and copies ran while one was open for 0% of the time, Pallas kernels for 1%

profile of v1, /device:TPU:7, one launch (start us, length us, event | category | flops | bytes accessed | tf_op | source)
XLA Modules:
  0.0 92.6 jit_solution(6332843754692417479)
XLA Ops:
  0.6 0.0 copy-start.6
  0.7 0.8 convert_multiply_fusion
  1.5 2.5 %collective-permute-start = (f32[8,128]{1,0:T(8,128)S(1)}, f32[8,128]{1,0:T(8,128)S(1)}, u32[]{:S(2)}, u32[]{:S(2)}) collective-permute-start(f32[8,128]{1,0:T(8,128)S(1)} %pad_maximum_fusion), channel_id=1, source_target_pairs={{0,1},{1,0},{2,3},{3,2},{4,5},{5,4},{6,7},{7,6},{8,9},{9,8},{10,11... | collective-permute-start | bytes 12296 | tf_op jit(solution)/shard_map/ppermute | solution.py:298
  4.0 8.0 %collective-permute-start.1 = (f32[8,128]{1,0:T(8,128)S(1)}, f32[8,128]{1,0:T(8,128)S(1)}, u32[]{:S(2)}, u32[]{:S(2)}) collective-permute-start(f32[8,128]{1,0:T(8,128)S(1)} %pad_maximum_fusion.1), channel_id=1, source_target_pairs={{1,2},{2,1},{3,4},{4,3},{5,6},{6,5},{9,10},{10,9},{11,12},{12,11},... | collective-permute-start | bytes 12296 | tf_op jit(solution)/shard_map/ppermute | solution.py:298
  12.0 0.0 copy-start.8
  12.0 0.1 pad_add_fusion.par_ref
  12.1 0.6 copy-done.8
  12.7 0.0 copy-start.9
  12.7 0.1 copy.15.owner_ref
  12.8 0.6 copy-done.9
  13.4 0.0 copy-start.10
  13.4 0.1 copy.16.patch_ref
  13.5 0.6 copy-done.10
  14.1 0.1 copy.17.count_ref
  14.1 0.0 copy-done.6
  14.2 0.0 copy-start
  14.2 0.9 %copy-done = f32[512,128]{1,0:T(8,128)S(1)} copy-done((f32[512,128]{1,0:T(8,128)S(1)}, f32[512,128]{1,0:T(8,128)}, u32[]{:S(2)}) %copy-start) | copy-done | bytes 262168
  15.1 0.0 copy-start.2
  15.1 0.9 %copy-done.2 = f32[512,128]{1,0:T(8,128)S(1)} copy-done((f32[512,128]{1,0:T(8,128)S(1)}, f32[512,128]{1,0:T(8,128)}, u32[]{:S(2)}) %copy-start.2) | copy-done | bytes 262168
  16.1 0.0 copy-start.3
  16.1 0.9 %copy-done.3 = s32[512,128]{1,0:T(8,128)S(1)} copy-done((s32[512,128]{1,0:T(8,128)S(1)}, s32[512,128]{1,0:T(8,128)}, u32[]{:S(2)}) %copy-start.3) | copy-done | bytes 262168
  17.0 0.0 copy-start.1
  17.0 0.8 shard_map.113
  17.8 0.0 collective-permute-done.ra_ref.na_ref
  17.8 0.0 collective-permute-done.1.rb_ref.nb_ref
  17.8 0.0 copy-start.5
  17.8 0.7 shard_map.114
  18.5 3.2 %collective-permute-start.2 = (f32[8,640]{1,0:T(8,128)S(1)}, f32[8,640]{1,0:T(8,128)S(1)}, u32[]{:S(2)}, u32[]{:S(2)}) collective-permute-start(f32[8,640]{1,0:T(8,128)S(1)} %get-tuple-element.16), channel_id=1, source_target_pairs={{0,8},{8,0},{16,24},{24,16},{32,40},{40,32},{48,56},{56,48},{64,72... | collective-permute-start | bytes 61448 | tf_op jit(solution)/shard_map/ppermute | solution.py:298
  21.7 2.2 %collective-permute-start.3 = (f32[8,640]{1,0:T(8,128)S(1)}, f32[8,640]{1,0:T(8,128)S(1)}, u32[]{:S(2)}, u32[]{:S(2)}) collective-permute-start(f32[8,640]{1,0:T(8,128)S(1)} %get-tuple-element.17), channel_id=1, source_target_pairs={{8,16},{16,8},{24,32},{32,24},{40,48},{48,40},{56,64},{64,56},{72,... | collective-permute-start | bytes 61448 | tf_op jit(solution)/shard_map/ppermute | solution.py:298
  23.9 0.0 collective-permute-done.2.ea_ref
  23.9 2.9 %collective-permute-done.3.eb_ref = f32[8,640]{1,0:T(8,128)S(1)} collective-permute-done((f32[8,640]{1,0:T(8,128)S(1)}, f32[8,640]{1,0:T(8,128)S(1)}, u32[]{:S(2)}, u32[]{:S(2)}) %collective-permute-start.3) | collective-permute-done | bytes 20512 | tf_op jit(solution)/shard_map/ppermute | solution.py:298
  26.8 0.0 copy-done.1
  26.8 0.0 copy-done.5
  26.8 0.0 copy-start.4
  26.8 3.8 %shard_map.115 = (f32[512,128]{1,0:T(8,128)}, f32[128,128]{1,0:T(8,128)S(1)}) custom-call(s32[2]{0:T(128)S(1)} %pad_add_fusion.par_ref, f32[512,128]{1,0:T(8,128)S(1)} %copy-done.1, f32[512,128]{1,0:T(8,128)S(1)} %copy-done.2, s32[512,128]{1,0:T(8,128)S(1)} %copy-done.3, f32[8,128]{1,0:T(8,128)S(1)} %collective-permute-done.ra_ref.na_ref, ...), custom_call_target="tpu_custom_call" | custom-call | tf_op jit(solution)/shard_map/pallas_call | solution.py:274
  30.6 0.0 copy-start.7
  30.6 39.3 %all_to_all.22 = f32[128,1,128]{2,1,0:T(1,128)S(1)} all-to-all(f32[128,1,128]{2,1,0:T(1,128)S(1)} %bitcast.15), channel_id=1, replica_groups=mesh['lon'=128,'lat'=8] {'lon'}, dimensions={0} | all-to-all | bytes 131072 | tf_op jit(solution)/shard_map/all_to_all | solution.py:351
  69.9 0.0 copy-done.4
  69.9 0.0 copy-done.7
  69.9 1.2 %shard_map.116 = f32[128,128]{1,0:T(8,128)S(1)} custom-call(f32[128,128]{1,0:T(8,128)S(1)} %bitcast.12, f32[256,256]{1,0:T(8,128)S(1)} %bitcast.14, f32[32,32]{1,0:T(8,128)S(1)} %copy-done.7), custom_call_target="tpu_custom_call" | custom-call | tf_op jit(solution)/shard_map/pallas_call | solution.py:274
  71.1 20.0 %all_to_all.23 = f32[128,1,128]{2,1,0:T(1,128)S(1)} all-to-all(f32[128,1,128]{2,1,0:T(1,128)S(1)} %bitcast.13), channel_id=1, replica_groups=mesh['lon'=128,'lat'=8] {'lon'}, dimensions={0} | all-to-all | bytes 131072 | tf_op jit(solution)/shard_map/all_to_all | solution.py:357
  91.1 1.4 %shard_map.117 = f32[512,128]{1,0:T(8,128)} custom-call(f32[128,128]{1,0:T(8,128)S(1)} %bitcast.11, bf16[256,128]{1,0:T(8,128)(2,1)S(1)} %get-tuple-element.23.hot_t_ref, f32[256,128]{1,0:T(8,128)S(1)} %get-tuple-element.20.mask_ref, f32[512,128]{1,0:T(8,128)S(1)} %get-tuple-element.18.lat4_ref, f32[32,128]{1,0:T(8,128)S(1)} %copy-done.5), custom_call_target="tpu_custom_call" | custom-call | tf_op jit(solution)/shard_map/pallas_call | solution.py:274
  (2 shorter events, 0.0 us)
Async XLA Ops:
  0.6 13.5 %copy-start.6 = (f32[32,512]{1,0:T(8,128)S(1)}, f32[32,512]{1,0:T(8,128)}, u32[]{:S(2)}) copy-start(f32[32,512]{1,0:T(8,128)} %lat_ref.1) | copy-start | bytes 196612
  1.5 16.3 %collective-permute-start = (f32[8,128]{1,0:T(8,128)S(1)}, f32[8,128]{1,0:T(8,128)S(1)}, u32[]{:S(2)}, u32[]{:S(2)}) collective-permute-start(f32[8,128]{1,0:T(8,128)S(1)} %pad_maximum_fusion), channel_id=1, source_target_pairs={{0,1},{1,0},{2,3},{3,2},{4,5},{5,4},{6,7},{7,6},{8,9},{9,8},{10,11... | collective-permute-start | bytes 12296 | tf_op jit(solution)/shard_map/ppermute | solution.py:298
  4.0 13.8 %collective-permute-start.1 = (f32[8,128]{1,0:T(8,128)S(1)}, f32[8,128]{1,0:T(8,128)S(1)}, u32[]{:S(2)}, u32[]{:S(2)}) collective-permute-start(f32[8,128]{1,0:T(8,128)S(1)} %pad_maximum_fusion.1), channel_id=1, source_target_pairs={{1,2},{2,1},{3,4},{4,3},{5,6},{6,5},{9,10},{10,9},{11,12},{12,11},... | collective-permute-start | bytes 12296 | tf_op jit(solution)/shard_map/ppermute | solution.py:298
  12.0 0.7 copy-start.8
  12.7 0.7 copy-start.9
  13.4 0.7 copy-start.10
  14.2 1.0 %copy-start = (f32[512,128]{1,0:T(8,128)S(1)}, f32[512,128]{1,0:T(8,128)}, u32[]{:S(2)}) copy-start(f32[512,128]{1,0:T(8,128)} %h_ref.3) | copy-start | bytes 786436
  15.1 0.9 %copy-start.2 = (f32[512,128]{1,0:T(8,128)S(1)}, f32[512,128]{1,0:T(8,128)}, u32[]{:S(2)}) copy-start(f32[512,128]{1,0:T(8,128)} %d_ref.3) | copy-start | bytes 786436
  16.1 0.9 %copy-start.3 = (s32[512,128]{1,0:T(8,128)S(1)}, s32[512,128]{1,0:T(8,128)}, u32[]{:S(2)}) copy-start(s32[512,128]{1,0:T(8,128)} %w_ref.3) | copy-start | bytes 786436
  17.0 9.8 %copy-start.1 = (f32[512,128]{1,0:T(8,128)S(1)}, f32[512,128]{1,0:T(8,128)}, u32[]{:S(2)}) copy-start(f32[512,128]{1,0:T(8,128)} %h_ref.3) | copy-start | bytes 786436
  17.8 9.0 %copy-start.5 = (f32[32,128]{1,0:T(8,128)S(1)}, f32[32,128]{1,0:T(8,128)}, u32[]{:S(2)}) copy-start(f32[32,128]{1,0:T(8,128)} %lon_ref.3) | copy-start | bytes 49156
  18.5 5.4 %collective-permute-start.2 = (f32[8,640]{1,0:T(8,128)S(1)}, f32[8,640]{1,0:T(8,128)S(1)}, u32[]{:S(2)}, u32[]{:S(2)}) collective-permute-start(f32[8,640]{1,0:T(8,128)S(1)} %get-tuple-element.16), channel_id=1, source_target_pairs={{0,8},{8,0},{16,24},{24,16},{32,40},{40,32},{48,56},{56,48},{64,72... | collective-permute-start | bytes 61448 | tf_op jit(solution)/shard_map/ppermute | solution.py:298
  21.7 5.1 %collective-permute-start.3 = (f32[8,640]{1,0:T(8,128)S(1)}, f32[8,640]{1,0:T(8,128)S(1)}, u32[]{:S(2)}, u32[]{:S(2)}) collective-permute-start(f32[8,640]{1,0:T(8,128)S(1)} %get-tuple-element.17), channel_id=1, source_target_pairs={{8,16},{16,8},{24,32},{32,24},{40,48},{48,40},{56,64},{64,56},{72,... | collective-permute-start | bytes 61448 | tf_op jit(solution)/shard_map/ppermute | solution.py:298
  26.8 43.1 %copy-start.4 = (f32[1,1,256,256]{3,2,1,0:T(8,128)S(1)}, f32[1,1,256,256]{3,2,1,0:T(8,128)}, u32[]{:S(2)}) copy-start(f32[1,1,256,256]{3,2,1,0:T(8,128)} %param.18) | copy-start | bytes 786436
  30.6 39.3 %copy-start.7 = (f32[32,32]{1,0:T(8,128)S(1)}, f32[32,32]{1,0:T(8,128)}, u32[]{:S(2)}) copy-start(f32[32,32]{1,0:T(8,128)} %sub_ref.1) | copy-start | bytes 12292

commit v2 on v1

v2 whole, which is shorter than its diff:
```python
import jax
import jax.numpy as jnp
from jax import lax
from jax.experimental import pallas as pl
from jax.experimental.pallas import tpu as pltpu
from jax.sharding import PartitionSpec as P

STEPS = 4
RIM = 4
TS = 16
SUB = 32
NPATCH = 256
CAP = 3
EDGE = 16
WRITES = 4
COURANT = 0.6
LANES = 128
F32 = jnp.float32
BF16 = jnp.bfloat16


def iota(shape, dim):
    return lax.broadcasted_iota(jnp.int32, shape, dim)


def parts(x):
    high = x.astype(BF16)
    return high, (x - high.astype(F32)).astype(BF16)


def dot(a, b):
    return lax.dot_general(a, b, (((1,), (0,)), ((), ())), preferred_element_type=F32)


def dot_t(a, b):
    return lax.dot_general(a, b, (((1,), (1,)), ((), ())), preferred_element_type=F32)


def one_hot_dot(hot, x):
    high, low = parts(x)
    return dot(hot, high) + dot(hot, low)


def dot3(a, b, product=dot):
    a_high, a_low = parts(a)
    b_high, b_low = parts(b)
    return product(a_high, b_high) + (product(a_high, b_low) + product(a_low, b_high))


def spread_lon(basis_lon):
    tiles = LANES // TS
    tall = jnp.concatenate([basis_lon] * tiles, axis=0)
    inside = iota(tall.shape, 0) // SUB == iota(tall.shape, 1) // TS
    return jnp.where(inside, tall, 0.0)


def edge_columns(height, wet_depth):
    lane = iota(height.shape, 1)
    near = jnp.where(lane < EDGE, height, pltpu.roll(wet_depth, EDGE, 1))
    far = jnp.where(lane >= LANES - EDGE, height, pltpu.roll(wet_depth, LANES - EDGE, 1))
    return jnp.where(lane < LANES // 2, near, far)


def fetch(pairs, sems):
    copies = [pltpu.make_async_copy(src, dst, sems.at[i]) for i, (src, dst) in enumerate(pairs)]
    for copy in copies:
        copy.start()
    for copy in copies:
        copy.wait()


def prepare(h_ref, d_ref, w_ref, height_ref, wet_depth_ref, edge_ref, depth_buf, wet_buf, sems):
    fetch([(h_ref, height_ref), (d_ref, depth_buf), (w_ref, wet_buf)], sems)
    wet_depth = depth_buf[...] * wet_buf[...].astype(F32)
    wet_depth_ref[...] = wet_depth
    edge_ref[...] = edge_columns(height_ref[...], wet_depth).T


def tables(lat_ref, lon_ref, owner_ref, patch_ref, count_ref,
           lat4_ref, lon_high_ref, lon_low_ref, hot_ref, hot_t_ref, mask_ref):
    lat4_ref[...] = jnp.concatenate([lat_ref[...]] * 4, axis=0).T
    lon_high_ref[...], lon_low_ref[...] = parts(spread_lon(lon_ref[...]))

    def column(ref):
        table = ref[...].astype(F32).T
        flat = jnp.concatenate([table[:, k:k + 1] for k in range(table.shape[1])], axis=0)
        return jnp.broadcast_to(flat, (flat.shape[0], LANES))

    owner = column(owner_ref)
    patch = column(patch_ref)
    count = column(count_ref)
    owner_row = owner.T
    total = owner.shape[0]
    hot_t_ref[...] = (owner == iota(owner.shape, 1).astype(F32)).astype(BF16)
    hot_ref[...] = (owner_row == iota(owner_row.shape, 0).astype(F32)).astype(BF16)
    rank = jnp.zeros((total, LANES), F32)
    for q in range(total // LANES):
        row = jnp.broadcast_to(owner_row[0:1, q * LANES:(q + 1) * LANES], (total, LANES))
        earlier = iota((total, LANES), 1) + q * LANES < iota((total, LANES), 0)
        rank = rank + jnp.where(earlier & (row == owner), 1.0, 0.0)
    rank = jnp.broadcast_to(jnp.sum(rank, axis=1, keepdims=True), (total, LANES))
    lane = iota((total, LANES), 1)
    group = (lane // SUB).astype(F32)
    place = (lane % SUB).astype(F32)
    live = jnp.where((rank == group) & (place < count), 1.0, 0.0)
    number = jnp.where(rank == place, patch, 0.0)
    mask_ref[...] = jnp.where(lane < CAP * SUB, live, number)


def rims(parity_lat, ra, rb):
    south = jnp.where(parity_lat == 0, ra, rb)
    north = jnp.where(parity_lat == 0, rb, ra)
    return north, south


def corners(par_ref, edge_ref, ra_ref, rb_ref, first_ref, second_ref, strip_ref):
    north, south = rims(par_ref[1], ra_ref[...], rb_ref[...])
    block = jnp.concatenate(
        [
            edge_columns(south[0:8], south[8:16]),
            jnp.zeros((LANES - 16, LANES), F32),
            edge_columns(north[0:8], north[8:16]),
        ],
        axis=0,
    ).T
    rows = edge_ref.shape[1]
    strip_ref[0:2 * EDGE, 0:rows] = edge_ref[0:2 * EDGE, :]
    strip_ref[2 * EDGE:, 0:rows] = edge_ref[LANES - 2 * EDGE:, :]
    strip_ref[0:2 * EDGE, rows:] = block[0:2 * EDGE]
    strip_ref[2 * EDGE:, rows:] = block[LANES - 2 * EDGE:]
    west = jnp.concatenate([strip_ref[0:RIM, :], strip_ref[EDGE:EDGE + RIM, :]], axis=0)
    east = jnp.concatenate(
        [strip_ref[4 * EDGE - RIM:, :], strip_ref[3 * EDGE - RIM:3 * EDGE, :]], axis=0
    )
    first_ref[...] = jnp.where(par_ref[0] == 0, east, west)
    second_ref[...] = jnp.where(par_ref[0] == 0, west, east)


def march(height, wet_depth, right, below):
    def ahead(x, dim):
        return pltpu.roll(x, x.shape[dim] - 1, dim)

    ce = COURANT * jnp.minimum(wet_depth, ahead(wet_depth, right))
    cn = COURANT * jnp.minimum(wet_depth, ahead(wet_depth, below))
    east = jnp.zeros_like(height)
    north = jnp.zeros_like(height)
    for _ in range(STEPS):
        east = east + ce * (ahead(height, right) - height)
        north = north + cn * (ahead(height, below) - height)
        height = (
            height
            + COURANT * (east - pltpu.roll(east, 1, right))
            + COURANT * (north - pltpu.roll(north, 1, below))
        )
    return height


def inner(par_ref, height_ref, wet_depth_ref, ra_ref, rb_ref, out_ref):
    north, south = rims(par_ref[1], ra_ref[...], rb_ref[...])
    height = jnp.concatenate([north[0:8], height_ref[...], south[0:8]], axis=0)
    wet_depth = jnp.concatenate([north[8:16], wet_depth_ref[...], south[8:16]], axis=0)
    out_ref[...] = march(height, wet_depth, 1, 0)[8:8 + out_ref.shape[0]]


def forward(par_ref, inner_ref, strip_ref, ea_ref, eb_ref, lat4_ref, lon_high_ref, lon_low_ref,
            hot_ref, mask_ref, out_ref, send_ref, final_buf, sem):
    rows_own = inner_ref.shape[0]
    from_east = jnp.where(par_ref[0] == 0, ea_ref[...], eb_ref[...])
    from_west = jnp.where(par_ref[0] == 0, eb_ref[...], ea_ref[...])
    keep = EDGE - RIM
    west = march(
        jnp.concatenate([from_west[0:RIM], strip_ref[0:keep, :]], axis=0),
        jnp.concatenate([from_west[RIM:], strip_ref[EDGE:EDGE + keep, :]], axis=0),
        0, 1,
    )
    east = march(
        jnp.concatenate([strip_ref[3 * EDGE + RIM:, :], from_east[0:RIM]], axis=0),
        jnp.concatenate([strip_ref[2 * EDGE + RIM:3 * EDGE, :], from_east[RIM:]], axis=0),
        0, 1,
    )
    lanes = west.shape[1]
    table = jnp.concatenate(
        [west[RIM:2 * RIM], jnp.zeros((LANES - 2 * RIM, lanes), F32), east[EDGE - 2 * RIM:EDGE - RIM]],
        axis=0,
    )[:, :rows_own].T
    lane = iota((rows_own, LANES), 1)
    final = jnp.where((lane < RIM) | (lane >= LANES - RIM), table, inner_ref[...])
    final_buf[...] = final
    write = pltpu.make_async_copy(final_buf, out_ref, sem)
    write.start()

    high, low = parts(final)
    product = dot_t(high, lon_high_ref[...]) + (
        dot_t(high, lon_low_ref[...]) + dot_t(low, lon_high_ref[...])
    )
    lat4 = lat4_ref[...]
    product = product * jnp.concatenate([lat4, lat4], axis=1)
    tile_rows = rows_own // TS
    sums = jnp.sum(product.reshape(tile_rows, TS, product.shape[1]), axis=1)
    group = iota((tile_rows, LANES), 1) // SUB
    stacked = []
    for q in range(sums.shape[1] // LANES):
        for g in range(4):
            own = jnp.where(group == g, sums[:, q * LANES:(q + 1) * LANES], 0.0)
            own = own + pltpu.roll(own, 2 * SUB, 1)
            stacked.append(own + pltpu.roll(own, SUB, 1))
    values = jnp.concatenate(stacked, axis=0)
    mask = mask_ref[...]
    filled = jnp.where(iota(mask.shape, 1) < CAP * SUB, values * mask, mask)
    send_ref[...] = one_hot_dot(hot_ref[...], filled)
    write.wait()


def smooth(recv_ref, prior_ref, sub_ref, reply_ref):
    received = recv_ref[...]
    turned = received.T
    devices = received.shape[0]
    group = iota((devices, LANES), 1) // SUB
    gathered = jnp.zeros((NPATCH, LANES), F32)
    for r in range(CAP):
        line = jnp.broadcast_to(turned[CAP * SUB + r:CAP * SUB + r + 1], (NPATCH, devices))
        member = (line == iota((NPATCH, devices), 0).astype(F32)).astype(BF16)
        gathered = gathered + one_hot_dot(member, jnp.where(group == r, received, 0.0))
    mixed = dot3(prior_ref[...], gathered)
    sub = jnp.concatenate([sub_ref[...]] * 4, axis=1)
    sub = jnp.concatenate([sub] * CAP + [jnp.zeros_like(sub)], axis=0)
    smoothed = dot3(mixed, sub)
    group = iota(smoothed.shape, 1) // SUB
    reply = jnp.zeros((devices, LANES), F32)
    for r in range(CAP):
        line = jnp.broadcast_to(received[:, CAP * SUB + r:CAP * SUB + r + 1], (devices, NPATCH))
        member = (line == iota((devices, NPATCH), 1).astype(F32)).astype(BF16)
        reply = reply + one_hot_dot(member, jnp.where(group == r, smoothed, 0.0))
    reply_ref[...] = reply


def backward(ret_ref, hot_t_ref, mask_ref, lat4_ref, lon_high_ref, lon_low_ref, out_ref, buf, sems):
    mask = mask_ref[...]
    picked = one_hot_dot(hot_t_ref[...], ret_ref[...])
    picked = jnp.where(iota(mask.shape, 1) < CAP * SUB, picked * mask, 0.0)
    picked = picked + pltpu.roll(picked, 2 * SUB, 1)
    picked = picked + pltpu.roll(picked, SUB, 1)
    rows = buf.shape[0]
    tile_rows = rows // TS
    group = iota((tile_rows, LANES), 1) // SUB
    halves = []
    for q in range(2):
        half = picked[4 * q * tile_rows:(4 * q + 1) * tile_rows]
        for g in range(1, 4):
            block = picked[(4 * q + g) * tile_rows:(4 * q + g + 1) * tile_rows]
            half = jnp.where(group == g, block, half)
        halves.append(half)
    value = jnp.concatenate(halves, axis=1)
    lon_high, lon_low = lon_high_ref[...], lon_low_ref[...]
    writes = []
    share = rows // WRITES
    for i in range(WRITES):
        part = value[i * share // TS:(i + 1) * share // TS]
        wide = jnp.broadcast_to(part[:, None, :], (share // TS, TS, part.shape[1]))
        lat4 = lat4_ref[i * share:(i + 1) * share, :]
        high, low = parts(wide.reshape(share, part.shape[1]) * jnp.concatenate([lat4, lat4], axis=1))
        buf[i * share:(i + 1) * share, :] = dot(high, lon_high) + (dot(high, lon_low) + dot(low, lon_high))
        span = pl.ds(i * share, share)
        writes.append(pltpu.make_async_copy(buf.at[span], out_ref.at[span], sems.at[i]))
        writes[-1].start()
    for write in writes:
        write.wait()


VMEM = pl.BlockSpec(memory_space=pltpu.VMEM)
SMEM = pl.BlockSpec(memory_space=pltpu.SMEM)
HBM = pl.BlockSpec(memory_space=pltpu.HBM)


def call(kernel, ins, outs, *args, scratch=()):
    return pl.pallas_call(
        kernel,
        out_shape=[jax.ShapeDtypeStruct(shape, dtype) for shape, dtype, _ in outs],
        in_specs=ins,
        out_specs=[spec for _, _, spec in outs],
        scratch_shapes=scratch,
        compiler_params=pltpu.CompilerParams(vmem_limit_bytes=32 * 1024 * 1024),
    )(*args)


def swap_pairs(axis, first, periodic):
    count = lax.axis_size(axis)
    pairs = []
    for a in range(first, count, 2):
        b = a + 1
        if b == count:
            if not periodic:
                continue
            b = 0
        pairs += [(a, b), (b, a)]
    return pairs


def swap(payload, axis, periodic):
    if axis == "lat":
        second = lax.ppermute(payload[1], axis, swap_pairs(axis, 1, periodic))
        late, _ = lax.optimization_barrier((payload[0], payload[1]))
        return lax.ppermute(late, axis, swap_pairs(axis, 0, periodic)), second
    late, _ = lax.optimization_barrier((payload[1], payload[0]))
    second = lax.ppermute(late, axis, swap_pairs(axis, 1, periodic))
    return lax.ppermute(payload[0], axis, swap_pairs(axis, 0, periodic)), second


def local(
    adjoint_height,
    depth,
    wet,
    basis_lat,
    basis_lon,
    tile_owner,
    tile_patch,
    tile_count,
    prior_patches,
    prior_subfaults,
):
    rows, cols = adjoint_height.shape
    lon_devices = lax.axis_size("lon")
    total = (rows // TS) * (cols // TS)
    parity = jnp.stack([lax.axis_index("lon") & 1, lax.axis_index("lat") & 1]).astype(jnp.int32)

    def edge_rows(start):
        def cut(x):
            return lax.dynamic_slice_in_dim(x, start, 8, axis=0)
        return jnp.concatenate([cut(adjoint_height), cut(depth) * cut(wet).astype(F32)], axis=0)

    last = (rows - 8) * (1 - parity[1])
    north_a, north_b = swap([edge_rows(last), edge_rows(rows - 8 - last)], "lat", False)
    dma = pltpu.SemaphoreType.DMA
    own = pltpu.VMEM((rows, cols), F32)
    height, wet_depth, edges = call(
        prepare,
        [HBM] * 3,
        [((rows, cols), F32, VMEM), ((rows, cols), F32, VMEM), ((LANES, rows), F32, VMEM)],
        *[pltpu.with_memory_space_constraint(x, pltpu.HBM) for x in (adjoint_height, depth, wet)],
        scratch=[own, pltpu.VMEM((rows, cols), jnp.int32), dma((3,))],
    )
    lat4, lon_high, lon_low, hot, hot_t, mask = call(
        tables,
        [VMEM] * 5,
        [
            ((rows, LANES), F32, VMEM),
            ((total, LANES), BF16, VMEM),
            ((total, LANES), BF16, VMEM),
            ((lon_devices, total), BF16, VMEM),
            ((total, lon_devices), BF16, VMEM),
            ((total, LANES), F32, VMEM),
        ],
        basis_lat, basis_lon, tile_owner.T, tile_patch.T, tile_count.T,
    )
    first, second, strips = call(
        corners,
        [SMEM] + [VMEM] * 3,
        [((2 * RIM, rows + LANES), F32, VMEM)] * 2 + [((4 * EDGE, rows + LANES), F32, VMEM)],
        parity, edges, north_a, north_b,
    )
    east_a, east_b = swap([first, second], "lon", True)
    (middle,) = call(
        inner, [SMEM] + [VMEM] * 4, [((rows, cols), F32, VMEM)],
        parity, height, wet_depth, north_a, north_b,
    )
    final, sent = call(
        forward,
        [SMEM] + [VMEM] * 9,
        [((rows, cols), F32, HBM), ((lon_devices, LANES), F32, VMEM)],
        parity, middle, strips, east_a, east_b, lat4, lon_high, lon_low, hot, mask,
        scratch=[own, dma(())],
    )
    received = lax.all_to_all(sent, "lon", split_axis=0, concat_axis=0, tiled=True)
    (replies,) = call(
        smooth,
        [VMEM] * 3,
        [((lon_devices, LANES), F32, VMEM)],
        received, prior_patches.reshape(NPATCH, NPATCH), prior_subfaults,
    )
    returned = lax.all_to_all(replies, "lon", split_axis=0, concat_axis=0, tiled=True)
    (gradient,) = call(
        backward,
        [VMEM] * 6,
        [((rows, cols), F32, HBM)],
        returned, hot_t, mask, lat4, lon_high, lon_low,
        scratch=[own, dma((WRITES,))],
    )
    return (final, gradient)


def solution(mesh):
    return jax.shard_map(
        local,
        mesh=mesh,
        in_specs=(
            P("lat", "lon"),
            P("lat", "lon"),
            P("lat", "lon"),
            P(None, "lat"),
            P(None, "lon"),
            P("lat", "lon"),
            P("lat", "lon"),
            P("lat", "lon"),
            P("lat", "lon", None, None),
            P(),
        ),
        out_specs=(P("lat", "lon"), P("lat", "lon")),
        check_vma=False,
    )
```

time: 93.1 us -> 86.8 us (0.932)
  blocking collectives: 59.3 us -> 43 us
  starting transfers between devices: 15.8 us -> 31.3 us
  local copies, waits for them, and re-layouts: 4.92 us -> 0.04 us
  waiting for transfers between devices: 2.89 us -> 1.02 us
  Pallas kernels: 7.96 us -> 9.44 us
    all_to_all x1, blocking collectives: 39.3 us -> 23 us  [local(): lax.all_to_all(sent, 'lon', split_axis=0, concat_axis=0, tiled=True)]
    ppermute x4, starting transfers between devices: 15.8 us -> 31.3 us  [the longest x1 17.6 us: swap(): lax.ppermute(payload[0], axis, swap_pairs(axis, 0, periodic))]
    unnamed x25 -> x14, local copies, waits for them, and re-layouts: 4.92 us -> 0.04 us
    ppermute x4, waiting for transfers between devices: 2.89 us -> 1.02 us  [the longest x1 1.01 us: swap(): return (lax.ppermute(late, axis, swap_pairs(axis, 0, periodic)), second)]
    pallas_call x5 -> x7, Pallas kernels: 7.96 us -> 9.44 us  [call(): pl.pallas_call(kernel, out_shape=[jax.ShapeDtypeStruct(shape, dtype) for...]
  transfers between devices with their start and end apart: 4 -> 4, of which waited for: 1 -> 1; matrix products, arithmetic and copies ran while one was open for 0% -> 0% of each run, Pallas kernels for 1% -> 4%
where the time goes in v2:
time: 86.8 us; the launch traced here: 86.4 us
  blocking collectives  43 us (50%)
  starting transfers between devices  31.3 us (36%)
  Pallas kernels  9.44 us (11%)
  waiting for transfers between devices  1.02 us (1%)
    all_to_all x1, blocking collectives, local(): lax.all_to_all(sent, 'lon', split_axis=0, concat_axis=0, tiled=True)  23 us
    all_to_all x1, blocking collectives, local(): lax.all_to_all(replies, 'lon', split_axis=0, concat_axis=0, tiled=True)  20 us
    ppermute x1, starting transfers between devices, swap(): lax.ppermute(payload[0], axis, swap_pairs(axis, 0, periodic))  17.6 us
    pallas_call x7, Pallas kernels, call(): pl.pallas_call(kernel, out_shape=[jax.ShapeDtypeStruct(shape, dtype) for...  9.44 us
    ppermute x1, starting transfers between devices, swap(): second = lax.ppermute(payload[1], axis, swap_pairs(axis, 1, periodic))  7.36 us
    ppermute x1, starting transfers between devices, swap(): second = lax.ppermute(late, axis, swap_pairs(axis, 1, periodic))  4.37 us
    ppermute x1, starting transfers between devices, swap(): return (lax.ppermute(late, axis, swap_pairs(axis, 0, periodic)), second)  1.92 us
  transfers between devices with their start and end apart: 4, of which 1 were waited for; matrix products, arithmetic and copies ran while one was open for 0% of the time, Pallas kernels for 4%

profile of v2, /device:TPU:7, one launch (start us, length us, event | category | flops | bytes accessed | tf_op | source)
XLA Modules:
  0.0 86.4 jit_solution(6598939917030708703)
XLA Ops:
  0.6 0.8 convert_multiply_fusion
  1.4 7.4 %collective-permute-start.1 = (f32[16,128]{1,0:T(8,128)S(1)}, f32[16,128]{1,0:T(8,128)S(1)}, u32[]{:S(2)}, u32[]{:S(2)}) collective-permute-start(f32[16,128]{1,0:T(8,128)S(1)} %pad_maximum_fusion.1), channel_id=1, source_target_pairs={{1,2},{2,1},{3,4},{4,3},{5,6},{6,5},{9,10},{10,9},{11,12},{12,11},... | collective-permute-start | bytes 24584 | tf_op jit(solution)/shard_map/ppermute | solution.py:301
  8.8 1.9 %collective-permute-start = (f32[16,128]{1,0:T(8,128)S(1)}, f32[16,128]{1,0:T(8,128)S(1)}, u32[]{:S(2)}, u32[]{:S(2)}) collective-permute-start(f32[16,128]{1,0:T(8,128)S(1)} %pad_maximum_fusion), channel_id=1, source_target_pairs={{0,1},{1,0},{2,3},{3,2},{4,5},{5,4},{6,7},{7,6},{8,9},{9,8},{10,11... | collective-permute-start | bytes 24584 | tf_op jit(solution)/shard_map/ppermute | solution.py:303
  10.7 0.1 pad_add_fusion.par_ref
  10.8 1.4 %shard_map.113 = (f32[512,128]{1,0:T(8,128)S(1)}, f32[512,128]{1,0:T(8,128)S(1)}, f32[128,512]{1,0:T(8,128)S(1)}) custom-call(f32[512,128]{1,0:T(8,128)} %h_ref.1, f32[512,128]{1,0:T(8,128)} %d_ref.1, s32[512,128]{1,0:T(8,128)} %w_ref.1), custom_call_target="tpu_custom_call" | custom-call | tf_op jit(solution)/shard_map/pallas_call | solution.py:276
  12.2 1.0 %collective-permute-done.ra_ref = f32[16,128]{1,0:T(8,128)S(1)} collective-permute-done((f32[16,128]{1,0:T(8,128)S(1)}, f32[16,128]{1,0:T(8,128)S(1)}, u32[]{:S(2)}, u32[]{:S(2)}) %collective-permute-start) | collective-permute-done | bytes 8224 | tf_op jit(solution)/shard_map/ppermute | solution.py:303
  13.3 0.0 collective-permute-done.1.rb_ref
  13.3 0.0 copy-start.1
  13.3 0.0 copy-start.3
  13.3 0.0 copy-start.6
  13.3 0.7 shard_map.115
  14.0 0.0 copy-start.5
  14.0 0.0 copy-start.4
  14.0 4.4 %collective-permute-start.3 = (f32[8,640]{1,0:T(8,128)S(1)}, f32[8,640]{1,0:T(8,128)S(1)}, u32[]{:S(2)}, u32[]{:S(2)}) collective-permute-start(f32[8,640]{1,0:T(8,128)S(1)} %get-tuple-element.25), channel_id=1, source_target_pairs={{8,16},{16,8},{24,32},{32,24},{40,48},{48,40},{56,64},{64,56},{72,... | collective-permute-start | bytes 61448 | tf_op jit(solution)/shard_map/ppermute | solution.py:305
  18.4 17.6 %collective-permute-start.2 = (f32[8,640]{1,0:T(8,128)S(1)}, f32[8,640]{1,0:T(8,128)S(1)}, u32[]{:S(2)}, u32[]{:S(2)}) collective-permute-start(f32[8,640]{1,0:T(8,128)S(1)} %get-tuple-element.23), channel_id=1, source_target_pairs={{0,8},{8,0},{16,24},{24,16},{32,40},{40,32},{48,56},{56,48},{64,72... | collective-permute-start | bytes 61448 | tf_op jit(solution)/shard_map/ppermute | solution.py:306
  36.0 0.0 copy-done.1
  36.0 0.0 copy-done.3
  36.0 0.0 copy-done.6
  36.0 0.0 copy-done.5
  36.0 0.0 copy-done.4
  36.1 0.7 shard_map.116
  36.8 1.3 %shard_map.114.inner_ref = f32[512,128]{1,0:T(8,128)S(1)} custom-call(s32[2]{0:T(128)S(1)} %pad_add_fusion.par_ref, f32[512,128]{1,0:T(8,128)S(1)} %get-tuple-element.18.height_ref, f32[512,128]{1,0:T(8,128)S(1)} %get-tuple-element.19.wet_depth_ref, f32[16,128]{1,0:T(8,128)S(1)} %collective-permute-done.ra_ref, f32[16,128]{1,0:T(8,128)S(1)} %collective-permute-done.1.rb_ref), custom_call_target="tpu_custom_call" | custom-call | tf_op jit(solution)/shard_map/pallas_call | solution.py:276
  38.1 0.0 collective-permute-done.3.eb_ref
  38.1 0.0 collective-permute-done.2.ea_ref
  38.2 0.0 copy-start
  38.2 2.6 %shard_map.117 = (f32[512,128]{1,0:T(8,128)}, f32[128,128]{1,0:T(8,128)S(1)}) custom-call(s32[2]{0:T(128)S(1)} %pad_add_fusion.par_ref, f32[512,128]{1,0:T(8,128)S(1)} %shard_map.114.inner_ref, f32[64,640]{1,0:T(8,128)S(1)} %get-tuple-element.22.strip_ref, f32[8,640]{1,0:T(8,128)S(1)} %collective-permute-done.2.ea_ref, ...), custom_call_target="tpu_custom_call" | custom-call | tf_op jit(solution)/shard_map/pallas_call | solution.py:276
  40.7 0.0 copy-start.2
  40.7 23.0 %all_to_all.22 = f32[128,1,128]{2,1,0:T(1,128)S(1)} all-to-all(f32[128,1,128]{2,1,0:T(1,128)S(1)} %bitcast.18), channel_id=1, replica_groups=mesh['lon'=128,'lat'=8] {'lon'}, dimensions={0} | all-to-all | bytes 131072 | tf_op jit(solution)/shard_map/all_to_all | solution.py:373
  63.7 0.0 copy-done
  63.7 0.0 copy-done.2
  63.8 1.2 %shard_map.118 = f32[128,128]{1,0:T(8,128)S(1)} custom-call(f32[128,128]{1,0:T(8,128)S(1)} %bitcast.15, f32[256,256]{1,0:T(8,128)S(1)} %bitcast.17, f32[32,32]{1,0:T(8,128)S(1)} %copy-done.2), custom_call_target="tpu_custom_call" | custom-call | tf_op jit(solution)/shard_map/pallas_call | solution.py:276
  65.0 20.0 %all_to_all.23 = f32[128,1,128]{2,1,0:T(1,128)S(1)} all-to-all(f32[128,1,128]{2,1,0:T(1,128)S(1)} %bitcast.16), channel_id=1, replica_groups=mesh['lon'=128,'lat'=8] {'lon'}, dimensions={0} | all-to-all | bytes 131072 | tf_op jit(solution)/shard_map/all_to_all | solution.py:380
  85.0 1.5 %shard_map.119 = f32[512,128]{1,0:T(8,128)} custom-call(f32[128,128]{1,0:T(8,128)S(1)} %bitcast.14, bf16[256,128]{1,0:T(8,128)(2,1)S(1)} %get-tuple-element.33.hot_t_ref, f32[256,128]{1,0:T(8,128)S(1)} %get-tuple-element.30.mask_ref, f32[512,128]{1,0:T(8,128)S(1)} %get-tuple-element.26.lat4_ref, bf16[256,128]{1,0:T(8,128)(2,1)S(1)} %get-tuple-element.27.lon_high_ref, ...), custom_call_target="tpu_custom_call" | custom-call | tf_op jit(solution)/shard_map/pallas_call | solution.py:276
  (2 shorter events, 0.0 us)
Async XLA Ops:
  1.4 11.8 %collective-permute-start.1 = (f32[16,128]{1,0:T(8,128)S(1)}, f32[16,128]{1,0:T(8,128)S(1)}, u32[]{:S(2)}, u32[]{:S(2)}) collective-permute-start(f32[16,128]{1,0:T(8,128)S(1)} %pad_maximum_fusion.1), channel_id=1, source_target_pairs={{1,2},{2,1},{3,4},{4,3},{5,6},{6,5},{9,10},{10,9},{11,12},{12,11},... | collective-permute-start | bytes 24584 | tf_op jit(solution)/shard_map/ppermute | solution.py:301
  8.8 4.5 %collective-permute-start = (f32[16,128]{1,0:T(8,128)S(1)}, f32[16,128]{1,0:T(8,128)S(1)}, u32[]{:S(2)}, u32[]{:S(2)}) collective-permute-start(f32[16,128]{1,0:T(8,128)S(1)} %pad_maximum_fusion), channel_id=1, source_target_pairs={{0,1},{1,0},{2,3},{3,2},{4,5},{5,4},{6,7},{7,6},{8,9},{9,8},{10,11... | collective-permute-start | bytes 24584 | tf_op jit(solution)/shard_map/ppermute | solution.py:303
  13.3 22.8 %copy-start.1 = (f32[32,512]{1,0:T(8,128)S(1)}, f32[32,512]{1,0:T(8,128)}, u32[]{:S(2)}) copy-start(f32[32,512]{1,0:T(8,128)} %lat_ref.1) | copy-start | bytes 196612
  13.3 22.8 %copy-start.3 = (f32[32,128]{1,0:T(8,128)S(1)}, f32[32,128]{1,0:T(8,128)}, u32[]{:S(2)}) copy-start(f32[32,128]{1,0:T(8,128)} %lon_ref.1) | copy-start | bytes 49156
  13.3 22.8 %copy-start.6 = (s32[32,8]{0,1:T(8,128)S(1)}, s32[32,8]{0,1:T(8,128)}, u32[]{:S(2)}) copy-start(s32[32,8]{0,1:T(8,128)} %param.17) | copy-start | bytes 3076
  14.0 22.0 %copy-start.5 = (s32[32,8]{0,1:T(8,128)S(1)}, s32[32,8]{0,1:T(8,128)}, u32[]{:S(2)}) copy-start(s32[32,8]{0,1:T(8,128)} %param.16) | copy-start | bytes 3076
  14.0 22.0 %copy-start.4 = (s32[32,8]{0,1:T(8,128)S(1)}, s32[32,8]{0,1:T(8,128)}, u32[]{:S(2)}) copy-start(s32[32,8]{0,1:T(8,128)} %param.15) | copy-start | bytes 3076
  14.0 24.1 %collective-permute-start.3 = (f32[8,640]{1,0:T(8,128)S(1)}, f32[8,640]{1,0:T(8,128)S(1)}, u32[]{:S(2)}, u32[]{:S(2)}) collective-permute-start(f32[8,640]{1,0:T(8,128)S(1)} %get-tuple-element.25), channel_id=1, source_target_pairs={{8,16},{16,8},{24,32},{32,24},{40,48},{48,40},{56,64},{64,56},{72,... | collective-permute-start | bytes 61448 | tf_op jit(solution)/shard_map/ppermute | solution.py:305
  18.4 19.8 %collective-permute-start.2 = (f32[8,640]{1,0:T(8,128)S(1)}, f32[8,640]{1,0:T(8,128)S(1)}, u32[]{:S(2)}, u32[]{:S(2)}) collective-permute-start(f32[8,640]{1,0:T(8,128)S(1)} %get-tuple-element.23), channel_id=1, source_target_pairs={{0,8},{8,0},{16,24},{24,16},{32,40},{40,32},{48,56},{56,48},{64,72... | collective-permute-start | bytes 61448 | tf_op jit(solution)/shard_map/ppermute | solution.py:306
  38.2 25.6 %copy-start = (f32[1,1,256,256]{3,2,1,0:T(8,128)S(1)}, f32[1,1,256,256]{3,2,1,0:T(8,128)}, u32[]{:S(2)}) copy-start(f32[1,1,256,256]{3,2,1,0:T(8,128)} %param.18) | copy-start | bytes 786436
  40.7 23.0 %copy-start.2 = (f32[32,32]{1,0:T(8,128)S(1)}, f32[32,32]{1,0:T(8,128)}, u32[]{:S(2)}) copy-start(f32[32,32]{1,0:T(8,128)} %sub_ref.1) | copy-start | bytes 12292

commit v3 on v2

v3 whole, which is shorter than its diff:
```python
import jax
import jax.numpy as jnp
from jax import lax
from jax.experimental import pallas as pl
from jax.experimental.pallas import tpu as pltpu
from jax.sharding import PartitionSpec as P

STEPS = 4
RIM = 4
TS = 16
SUB = 32
NPATCH = 256
CAP = 3
EDGE = 8
WRITES = 4
COURANT = 0.6
LANES = 128
F32 = jnp.float32
BF16 = jnp.bfloat16


def iota(shape, dim):
    return lax.broadcasted_iota(jnp.int32, shape, dim)


def parts(x):
    high = x.astype(BF16)
    return high, (x - high.astype(F32)).astype(BF16)


def dot(a, b):
    return lax.dot_general(a, b, (((1,), (0,)), ((), ())), preferred_element_type=F32)


def join_cols(*blocks):
    return jnp.concatenate(blocks, axis=1)


def join_rows(*blocks):
    return jnp.concatenate(blocks, axis=0)


def fold(x):
    return x[:, :LANES] + x[:, LANES:]


def spread_lon(basis_lon):
    tiles = LANES // TS
    tall = join_rows(*[basis_lon] * tiles)
    inside = iota(tall.shape, 0) // SUB == iota(tall.shape, 1) // TS
    return jnp.where(inside, tall, 0.0)


def edge_columns(height, wet_depth):
    lane = iota(height.shape, 1)
    near = jnp.where(lane < EDGE, height, pltpu.roll(wet_depth, EDGE, 1))
    far = jnp.where(lane >= LANES - EDGE, height, pltpu.roll(wet_depth, LANES - EDGE, 1))
    return jnp.where(lane < LANES // 2, near, far)


def pick_edges(turned):
    return join_rows(turned[0:2 * EDGE], turned[LANES - 2 * EDGE:])


def prepare(lat_hbm, lon_hbm, owner_hbm, patch_hbm, count_hbm, h_hbm, d_hbm, w_hbm,
            height_ref, wet_depth_ref, edge_ref, lat4_ref, lon_ref, lon_t_ref, hot_ref, hot_t_ref,
            mask_ref, lat_buf, lon_buf, owner_buf, patch_buf, count_buf, depth_buf, wet_buf, sems):
    pairs = [(lat_hbm, lat_buf), (lon_hbm, lon_buf), (owner_hbm, owner_buf), (patch_hbm, patch_buf),
             (count_hbm, count_buf), (h_hbm, height_ref), (d_hbm, depth_buf), (w_hbm, wet_buf)]
    copies = [pltpu.make_async_copy(src, dst, sems.at[i]) for i, (src, dst) in enumerate(pairs)]
    for copy in copies:
        copy.start()
    for copy in copies[:5]:
        copy.wait()
    lat4_ref[...] = join_rows(*[lat_buf[...]] * 4).T
    spread = spread_lon(lon_buf[...])
    lon_ref[...] = join_cols(*parts(spread))
    lon_t_ref[...] = join_rows(*parts(spread.T))

    def column(ref):
        table = ref[...].astype(F32).T
        flat = join_rows(*[table[:, k:k + 1] for k in range(table.shape[1])])
        return jnp.broadcast_to(flat, (flat.shape[0], LANES))

    owner = column(owner_buf)
    patch = column(patch_buf)
    count = column(count_buf)
    owner_row = owner.T
    total = owner.shape[0]
    hot_t = (owner == iota(owner.shape, 1).astype(F32)).astype(BF16)
    hot_t_ref[...] = join_cols(hot_t, hot_t)
    hot_ref[...] = (owner_row == iota(owner_row.shape, 0).astype(F32)).astype(BF16)
    rank = jnp.zeros((total, LANES), F32)
    for q in range(total // LANES):
        row = jnp.broadcast_to(owner_row[0:1, q * LANES:(q + 1) * LANES], (total, LANES))
        earlier = iota((total, LANES), 1) + q * LANES < iota((total, LANES), 0)
        rank = rank + jnp.where(earlier & (row == owner), 1.0, 0.0)
    rank = jnp.broadcast_to(jnp.sum(rank, axis=1, keepdims=True), (total, LANES))
    lane = iota((total, LANES), 1)
    group = (lane // SUB).astype(F32)
    place = (lane % SUB).astype(F32)
    live = jnp.where((rank == group) & (place < count), 1.0, 0.0)
    number = jnp.where(rank == place, patch, 0.0)
    mask_ref[...] = jnp.where(lane < CAP * SUB, live, number)

    for copy in copies[5:]:
        copy.wait()
    wet_depth = depth_buf[...] * wet_buf[...].astype(F32)
    wet_depth_ref[...] = wet_depth
    edge_ref[...] = pick_edges(edge_columns(height_ref[...], wet_depth).T)


def rims(parity_lat, ra, rb):
    south = jnp.where(parity_lat == 0, ra, rb)
    north = jnp.where(parity_lat == 0, rb, ra)
    return north, south


def corners(par_ref, edge_ref, ra_ref, rb_ref, first_ref, second_ref, block_ref):
    north, south = rims(par_ref[1], ra_ref[...], rb_ref[...])
    block = join_rows(
        edge_columns(south[0:8], south[8:16]),
        jnp.zeros((LANES - 16, LANES), F32),
        edge_columns(north[0:8], north[8:16]),
    ).T
    block = pick_edges(block)
    block_ref[...] = block
    strips = join_cols(edge_ref[...], block)
    west = join_rows(strips[0:RIM], strips[EDGE:EDGE + RIM])
    east = join_rows(strips[4 * EDGE - RIM:], strips[3 * EDGE - RIM:3 * EDGE])
    first_ref[...] = jnp.where(par_ref[0] == 0, east, west)
    second_ref[...] = jnp.where(par_ref[0] == 0, west, east)


def march(height, wet_depth, right, below):
    def ahead(x, dim):
        return pltpu.roll(x, x.shape[dim] - 1, dim)

    ce = COURANT * jnp.minimum(wet_depth, ahead(wet_depth, right))
    cn = COURANT * jnp.minimum(wet_depth, ahead(wet_depth, below))
    east = jnp.zeros_like(height)
    north = jnp.zeros_like(height)
    for _ in range(STEPS):
        east = east + ce * (ahead(height, right) - height)
        north = north + cn * (ahead(height, below) - height)
        height = (
            height
            + COURANT * (east - pltpu.roll(east, 1, right))
            + COURANT * (north - pltpu.roll(north, 1, below))
        )
    return height


def inner(par_ref, height_ref, wet_depth_ref, ra_ref, rb_ref, out_ref):
    north, south = rims(par_ref[1], ra_ref[...], rb_ref[...])
    height = join_rows(north[0:8], height_ref[...], south[0:8])
    wet_depth = join_rows(north[8:16], wet_depth_ref[...], south[8:16])
    out_ref[...] = march(height, wet_depth, 1, 0)[8:8 + out_ref.shape[0]]


def forward(par_ref, inner_ref, edge_ref, block_ref, ea_ref, eb_ref, lat4_ref, lon_t_ref,
            hot_ref, mask_ref, out_ref, send_ref, final_buf, sem):
    rows_own = inner_ref.shape[0]
    from_east = jnp.where(par_ref[0] == 0, ea_ref[...], eb_ref[...])
    from_west = jnp.where(par_ref[0] == 0, eb_ref[...], ea_ref[...])
    own = join_cols(edge_ref[...], block_ref[...])
    strip = march(
        join_rows(from_west[0:RIM], own[0:EDGE], own[3 * EDGE:], from_east[0:RIM]),
        join_rows(from_west[RIM:], own[EDGE:2 * EDGE], own[2 * EDGE:3 * EDGE], from_east[RIM:]),
        0, 1,
    )[:, :rows_own]
    table = join_rows(
        strip[RIM:2 * RIM], jnp.zeros((LANES - 2 * RIM, rows_own), F32), strip[2 * EDGE:2 * EDGE + RIM]
    ).T
    lane = iota((rows_own, LANES), 1)
    final = jnp.where((lane < RIM) | (lane >= LANES - RIM), table, inner_ref[...])
    final_buf[...] = final
    write = pltpu.make_async_copy(final_buf, out_ref, sem)
    write.start()

    high, low = parts(final)
    lon_high, lon_low = lon_t_ref[:LANES, :], lon_t_ref[LANES:, :]
    product = dot(join_cols(high, low), join_rows(lon_high, lon_high)) + dot(high, lon_low)
    lat4 = lat4_ref[...]
    product = product * join_cols(lat4, lat4)
    tile_rows = rows_own // TS
    sums = jnp.sum(product.reshape(tile_rows, TS, product.shape[1]), axis=1)
    group = iota((tile_rows, LANES), 1) // SUB
    stacked = []
    for q in range(sums.shape[1] // LANES):
        for g in range(4):
            part = jnp.where(group == g, sums[:, q * LANES:(q + 1) * LANES], 0.0)
            part = part + pltpu.roll(part, 2 * SUB, 1)
            stacked.append(part + pltpu.roll(part, SUB, 1))
    values = join_rows(*stacked)
    mask = mask_ref[...]
    filled = jnp.where(iota(mask.shape, 1) < CAP * SUB, values * mask, mask)
    send_ref[...] = fold(dot(hot_ref[...], join_cols(*parts(filled))))
    write.wait()


def smooth(recv_ref, prior_ref, sub_ref, reply_ref):
    received = recv_ref[...]
    turned = received.T
    devices = received.shape[0]
    group = iota((devices, 2 * LANES), 1) % LANES // SUB
    both = join_cols(*parts(received))

    def members(r):
        line = jnp.broadcast_to(turned[CAP * SUB + r:CAP * SUB + r + 1], (NPATCH, devices))
        return (line == iota((NPATCH, devices), 0).astype(F32)).astype(BF16)

    def share(r):
        return jnp.where(group == r, both, jnp.zeros_like(both))

    gathered = fold(
        dot(join_cols(members(0), members(1)), join_rows(share(0), share(1))) + dot(members(2), share(2))
    )
    prior_high, prior_low = parts(prior_ref[...])
    high, low = parts(gathered)
    mixed = fold(dot(prior_high, join_cols(high, low))) + dot(prior_low, high)
    sub = join_cols(*[sub_ref[...]] * 4)
    sub_high, sub_low = parts(join_rows(*[sub] * CAP, jnp.zeros_like(sub)))
    high, low = parts(mixed)
    smoothed = dot(join_cols(high, low), join_rows(sub_high, sub_high)) + dot(high, sub_low)
    both = join_cols(*parts(smoothed))
    group = iota((devices, LANES), 1) // SUB
    reply = None
    for r in range(CAP):
        line = jnp.broadcast_to(received[:, CAP * SUB + r:CAP * SUB + r + 1], (devices, NPATCH))
        member = (line == iota((devices, NPATCH), 1).astype(F32)).astype(BF16)
        found = fold(dot(member, both))
        reply = found if reply is None else jnp.where(group == r, found, reply)
    reply_ref[...] = reply


def backward(ret_ref, hot_t_ref, mask_ref, lat4_ref, lon_ref, out_ref, buf, sems):
    mask = mask_ref[...]
    picked = dot(hot_t_ref[...], join_rows(*parts(ret_ref[...])))
    picked = jnp.where(iota(mask.shape, 1) < CAP * SUB, picked * mask, 0.0)
    picked = picked + pltpu.roll(picked, 2 * SUB, 1)
    picked = picked + pltpu.roll(picked, SUB, 1)
    rows = buf.shape[0]
    tile_rows = rows // TS
    group = iota((tile_rows, LANES), 1) // SUB
    halves = []
    for q in range(2):
        half = picked[4 * q * tile_rows:(4 * q + 1) * tile_rows]
        for g in range(1, 4):
            block = picked[(4 * q + g) * tile_rows:(4 * q + g + 1) * tile_rows]
            half = jnp.where(group == g, block, half)
        halves.append(half)
    value = join_cols(*halves)
    lon = lon_ref[...]
    writes = []
    share = rows // WRITES
    for i in range(WRITES):
        part = value[i * share // TS:(i + 1) * share // TS]
        wide = jnp.broadcast_to(part[:, None, :], (share // TS, TS, part.shape[1]))
        lat4 = lat4_ref[i * share:(i + 1) * share, :]
        high, low = parts(wide.reshape(share, part.shape[1]) * join_cols(lat4, lat4))
        buf[i * share:(i + 1) * share, :] = fold(dot(high, lon)) + dot(low, lon[:, :LANES])
        span = pl.ds(i * share, share)
        writes.append(pltpu.make_async_copy(buf.at[span], out_ref.at[span], sems.at[i]))
        writes[-1].start()
    for write in writes:
        write.wait()


VMEM = pl.BlockSpec(memory_space=pltpu.VMEM)
SMEM = pl.BlockSpec(memory_space=pltpu.SMEM)
HBM = pl.BlockSpec(memory_space=pltpu.HBM)


def call(kernel, ins, outs, *args, scratch=()):
    return pl.pallas_call(
        kernel,
        out_shape=[jax.ShapeDtypeStruct(shape, dtype) for shape, dtype, _ in outs],
        in_specs=ins,
        out_specs=[spec for _, _, spec in outs],
        scratch_shapes=scratch,
        compiler_params=pltpu.CompilerParams(vmem_limit_bytes=32 * 1024 * 1024),
    )(*args)


def swap_pairs(axis, first, periodic):
    count = lax.axis_size(axis)
    pairs = []
    for a in range(first, count, 2):
        b = a + 1
        if b == count:
            if not periodic:
                continue
            b = 0
        pairs += [(a, b), (b, a)]
    return pairs


def swap(payload, axis, periodic):
    if axis == "lat":
        second = lax.ppermute(payload[1], axis, swap_pairs(axis, 1, periodic))
        late, _ = lax.optimization_barrier((payload[0], payload[1]))
        return lax.ppermute(late, axis, swap_pairs(axis, 0, periodic)), second
    late, _ = lax.optimization_barrier((payload[1], payload[0]))
    second = lax.ppermute(late, axis, swap_pairs(axis, 1, periodic))
    return lax.ppermute(payload[0], axis, swap_pairs(axis, 0, periodic)), second


def local(
    adjoint_height,
    depth,
    wet,
    basis_lat,
    basis_lon,
    tile_owner,
    tile_patch,
    tile_count,
    prior_patches,
    prior_subfaults,
):
    rows, cols = adjoint_height.shape
    lon_devices = lax.axis_size("lon")
    total = (rows // TS) * (cols // TS)
    parity = jnp.stack([lax.axis_index("lon") & 1, lax.axis_index("lat") & 1]).astype(jnp.int32)

    def edge_rows(start):
        def cut(x):
            return lax.dynamic_slice_in_dim(x, start, 8, axis=0)
        return jnp.concatenate([cut(adjoint_height), cut(depth) * cut(wet).astype(F32)], axis=0)

    last = (rows - 8) * (1 - parity[1])
    north_a, north_b = swap([edge_rows(last), edge_rows(rows - 8 - last)], "lat", False)
    dma = pltpu.SemaphoreType.DMA
    own = pltpu.VMEM((rows, cols), F32)
    tile_shape = (cols // TS, rows // TS)
    resident = [
        basis_lat, basis_lon, tile_owner.T, tile_patch.T, tile_count.T, adjoint_height, depth, wet
    ]
    height, wet_depth, edges, lat4, lon, lon_t, hot, hot_t, mask = call(
        prepare,
        [HBM] * len(resident),
        [
            ((rows, cols), F32, VMEM),
            ((rows, cols), F32, VMEM),
            ((4 * EDGE, rows), F32, VMEM),
            ((rows, LANES), F32, VMEM),
            ((total, 2 * LANES), BF16, VMEM),
            ((2 * LANES, total), BF16, VMEM),
            ((lon_devices, total), BF16, VMEM),
            ((total, 2 * lon_devices), BF16, VMEM),
            ((total, LANES), F32, VMEM),
        ],
        *[pltpu.with_memory_space_constraint(x, pltpu.HBM) for x in resident],
        scratch=[pltpu.VMEM((SUB, rows), F32), pltpu.VMEM((SUB, cols), F32)]
        + [pltpu.VMEM(tile_shape, jnp.int32)] * 3
        + [own, pltpu.VMEM((rows, cols), jnp.int32), dma((len(resident),))],
    )
    payload = ((2 * RIM, rows + LANES), F32, VMEM)
    first, second, block = call(
        corners,
        [SMEM] + [VMEM] * 3,
        [payload, payload, ((4 * EDGE, LANES), F32, VMEM)],
        parity, edges, north_a, north_b,
    )
    east_a, east_b = swap([first, second], "lon", True)
    (middle,) = call(
        inner, [SMEM] + [VMEM] * 4, [((rows, cols), F32, VMEM)],
        parity, height, wet_depth, north_a, north_b,
    )
    final, sent = call(
        forward,
        [SMEM] + [VMEM] * 9,
        [((rows, cols), F32, HBM), ((lon_devices, LANES), F32, VMEM)],
        parity, middle, edges, block, east_a, east_b, lat4, lon_t, hot, mask,
        scratch=[own, dma(())],
    )
    received = lax.all_to_all(sent, "lon", split_axis=0, concat_axis=0, tiled=True)
    (replies,) = call(
        smooth,
        [VMEM] * 3,
        [((lon_devices, LANES), F32, VMEM)],
        received, prior_patches.reshape(NPATCH, NPATCH), prior_subfaults,
    )
    returned = lax.all_to_all(replies, "lon", split_axis=0, concat_axis=0, tiled=True)
    (gradient,) = call(
        backward,
        [VMEM] * 5,
        [((rows, cols), F32, HBM)],
        returned, hot_t, mask, lat4, lon,
        scratch=[own, dma((WRITES,))],
    )
    return (final, gradient)


def solution(mesh):
    return jax.shard_map(
        local,
        mesh=mesh,
        in_specs=(
            P("lat", "lon"),
            P("lat", "lon"),
            P("lat", "lon"),
            P(None, "lat"),
            P(None, "lon"),
            P("lat", "lon"),
            P("lat", "lon"),
            P("lat", "lon"),
            P("lat", "lon", None, None),
            P(),
        ),
        out_specs=(P("lat", "lon"), P("lat", "lon")),
        check_vma=False,
    )
```

time: 86.8 us -> 85.1 us (0.980)
  Pallas kernels: 9.44 us -> 8.51 us
    pallas_call x7 -> x6, Pallas kernels: 9.44 us -> 8.51 us  [call(): pl.pallas_call(kernel, out_shape=[jax.ShapeDtypeStruct(shape, dtype) for...]
where the time goes in v3:
time: 85.1 us; the launch traced here: 84.7 us
  blocking collectives  43 us (51%)
  starting transfers between devices  31.1 us (37%)
  Pallas kernels  8.51 us (10%)
  other arithmetic  0.86 us (1%)
    all_to_all x1, blocking collectives, local(): lax.all_to_all(sent, 'lon', split_axis=0, concat_axis=0, tiled=True)  23 us
    all_to_all x1, blocking collectives, local(): lax.all_to_all(replies, 'lon', split_axis=0, concat_axis=0, tiled=True)  20 us
    ppermute x1, starting transfers between devices, swap(): lax.ppermute(payload[0], axis, swap_pairs(axis, 0, periodic))  17.6 us
    pallas_call x6, Pallas kernels, call(): pl.pallas_call(kernel, out_shape=[jax.ShapeDtypeStruct(shape, dtype) for...  8.51 us
    ppermute x1, starting transfers between devices, swap(): second = lax.ppermute(payload[1], axis, swap_pairs(axis, 1, periodic))  7.36 us
    ppermute x1, starting transfers between devices, swap(): second = lax.ppermute(late, axis, swap_pairs(axis, 1, periodic))  4.24 us
    ppermute x1, starting transfers between devices, swap(): return (lax.ppermute(late, axis, swap_pairs(axis, 0, periodic)), second)  1.92 us
  transfers between devices with their start and end apart: 4, of which 1 were waited for; matrix products, arithmetic and copies ran while one was open for 0% of the time, Pallas kernels for 4%

profile of v3, /device:TPU:7, one launch (start us, length us, event | category | flops | bytes accessed | tf_op | source)
XLA Modules:
  0.0 84.7 jit_solution(14878299720210215512)
XLA Ops:
  0.6 0.8 convert_multiply_fusion
  1.4 7.4 %collective-permute-start.1 = (f32[16,128]{1,0:T(8,128)S(1)}, f32[16,128]{1,0:T(8,128)S(1)}, u32[]{:S(2)}, u32[]{:S(2)}) collective-permute-start(f32[16,128]{1,0:T(8,128)S(1)} %pad_maximum_fusion.1), channel_id=1, source_target_pairs={{1,2},{2,1},{3,4},{4,3},{5,6},{6,5},{9,10},{10,9},{11,12},{12,11},... | collective-permute-start | bytes 24584 | tf_op jit(solution)/shard_map/ppermute | solution.py:301
  8.8 1.9 %collective-permute-start = (f32[16,128]{1,0:T(8,128)S(1)}, f32[16,128]{1,0:T(8,128)S(1)}, u32[]{:S(2)}, u32[]{:S(2)}) collective-permute-start(f32[16,128]{1,0:T(8,128)S(1)} %pad_maximum_fusion), channel_id=1, source_target_pairs={{0,1},{1,0},{2,3},{3,2},{4,5},{5,4},{6,7},{7,6},{8,9},{9,8},{10,11... | collective-permute-start | bytes 24584 | tf_op jit(solution)/shard_map/ppermute | solution.py:303
  10.7 0.1 pad_add_fusion.par_ref
  10.8 2.0 %shard_map.113 = (f32[512,128]{1,0:T(8,128)S(1)}, f32[512,128]{1,0:T(8,128)S(1)}, f32[32,512]{1,0:T(8,128)S(1)}, f32[512,128]{1,0:T(8,128)S(1)}, bf16[256,256]{1...) custom-call(f32[32,512]{1,0:T(8,128)} %lat_hbm.1, ...), custom_call_target="tpu_custom_call" | custom-call | tf_op jit(solution)/shard_map/pallas_call | solution.py:276
  12.8 0.4 collective-permute-done.ra_ref
  13.3 0.0 collective-permute-done.1.rb_ref
  13.3 0.7 shard_map.115
  14.0 4.2 %collective-permute-start.3 = (f32[8,640]{1,0:T(8,128)S(1)}, f32[8,640]{1,0:T(8,128)S(1)}, u32[]{:S(2)}, u32[]{:S(2)}) collective-permute-start(f32[8,640]{1,0:T(8,128)S(1)} %get-tuple-element.25), channel_id=1, source_target_pairs={{8,16},{16,8},{24,32},{32,24},{40,48},{48,40},{56,64},{64,56},{72,... | collective-permute-start | bytes 61448 | tf_op jit(solution)/shard_map/ppermute | solution.py:305
  18.2 17.6 %collective-permute-start.2 = (f32[8,640]{1,0:T(8,128)S(1)}, f32[8,640]{1,0:T(8,128)S(1)}, u32[]{:S(2)}, u32[]{:S(2)}) collective-permute-start(f32[8,640]{1,0:T(8,128)S(1)} %get-tuple-element.23), channel_id=1, source_target_pairs={{0,8},{8,0},{16,24},{24,16},{32,40},{40,32},{48,56},{56,48},{64,72... | collective-permute-start | bytes 61448 | tf_op jit(solution)/shard_map/ppermute | solution.py:306
  35.8 1.3 %shard_map.114.inner_ref = f32[512,128]{1,0:T(8,128)S(1)} custom-call(s32[2]{0:T(128)S(1)} %pad_add_fusion.par_ref, f32[512,128]{1,0:T(8,128)S(1)} %get-tuple-element.18.height_ref, f32[512,128]{1,0:T(8,128)S(1)} %get-tuple-element.19.wet_depth_ref, f32[16,128]{1,0:T(8,128)S(1)} %collective-permute-done.ra_ref, f32[16,128]{1,0:T(8,128)S(1)} %collective-permute-done.1.rb_ref), custom_call_target="tpu_custom_call" | custom-call | tf_op jit(solution)/shard_map/pallas_call | solution.py:276
  37.2 0.0 collective-permute-done.3.eb_ref
  37.2 0.0 collective-permute-done.2.ea_ref
  37.2 0.0 copy-start
  37.2 2.2 %shard_map.116 = (f32[512,128]{1,0:T(8,128)}, f32[128,128]{1,0:T(8,128)S(1)}) custom-call(s32[2]{0:T(128)S(1)} %pad_add_fusion.par_ref, f32[512,128]{1,0:T(8,128)S(1)} %shard_map.114.inner_ref, f32[32,512]{1,0:T(8,128)S(1)} %get-tuple-element.21.edge_ref, f32[32,128]{1,0:T(8,128)S(1)} %get-tuple-element.22.block_ref, ...), custom_call_target="tpu_custom_call" | custom-call | tf_op jit(solution)/shard_map/pallas_call | solution.py:276
  39.4 0.0 copy-start.1
  39.4 23.0 %all_to_all.22 = f32[128,1,128]{2,1,0:T(1,128)S(1)} all-to-all(f32[128,1,128]{2,1,0:T(1,128)S(1)} %bitcast.18), channel_id=1, replica_groups=mesh['lon'=128,'lat'=8] {'lon'}, dimensions={0} | all-to-all | bytes 131072 | tf_op jit(solution)/shard_map/all_to_all | solution.py:377
  62.4 0.0 copy-done
  62.4 0.0 copy-done.1
  62.4 0.9 %shard_map.117 = f32[128,128]{1,0:T(8,128)S(1)} custom-call(f32[128,128]{1,0:T(8,128)S(1)} %bitcast.14, f32[256,256]{1,0:T(8,128)S(1)} %bitcast.16, f32[32,32]{1,0:T(8,128)S(1)} %copy-done.1), custom_call_target="tpu_custom_call" | custom-call | tf_op jit(solution)/shard_map/pallas_call | solution.py:276
  63.4 20.0 %all_to_all.23 = f32[128,1,128]{2,1,0:T(1,128)S(1)} all-to-all(f32[128,1,128]{2,1,0:T(1,128)S(1)} %bitcast.15), channel_id=1, replica_groups=mesh['lon'=128,'lat'=8] {'lon'}, dimensions={0} | all-to-all | bytes 131072 | tf_op jit(solution)/shard_map/all_to_all | solution.py:384
  83.4 1.3 %shard_map.118 = f32[512,128]{1,0:T(8,128)} custom-call(f32[128,128]{1,0:T(8,128)S(1)} %bitcast.17, bf16[256,256]{1,0:T(8,128)(2,1)S(1)} %get-tuple-element.32.hot_t_ref, f32[256,128]{1,0:T(8,128)S(1)} %get-tuple-element.29.mask_ref, f32[512,128]{1,0:T(8,128)S(1)} %get-tuple-element.26.lat4_ref, bf16[256,256]{1,0:T(8,128)(2,1)S(1)} %get-tuple-element.33.lon_ref), custom_call_target="tpu_custom_call" | custom-call | tf_op jit(solution)/shard_map/pallas_call | solution.py:276
  (2 shorter events, 0.0 us)
Async XLA Ops:
  1.4 11.8 %collective-permute-start.1 = (f32[16,128]{1,0:T(8,128)S(1)}, f32[16,128]{1,0:T(8,128)S(1)}, u32[]{:S(2)}, u32[]{:S(2)}) collective-permute-start(f32[16,128]{1,0:T(8,128)S(1)} %pad_maximum_fusion.1), channel_id=1, source_target_pairs={{1,2},{2,1},{3,4},{4,3},{5,6},{6,5},{9,10},{10,9},{11,12},{12,11},... | collective-permute-start | bytes 24584 | tf_op jit(solution)/shard_map/ppermute | solution.py:301
  8.8 4.5 %collective-permute-start = (f32[16,128]{1,0:T(8,128)S(1)}, f32[16,128]{1,0:T(8,128)S(1)}, u32[]{:S(2)}, u32[]{:S(2)}) collective-permute-start(f32[16,128]{1,0:T(8,128)S(1)} %pad_maximum_fusion), channel_id=1, source_target_pairs={{0,1},{1,0},{2,3},{3,2},{4,5},{5,4},{6,7},{7,6},{8,9},{9,8},{10,11... | collective-permute-start | bytes 24584 | tf_op jit(solution)/shard_map/ppermute | solution.py:303
  14.0 23.2 %collective-permute-start.3 = (f32[8,640]{1,0:T(8,128)S(1)}, f32[8,640]{1,0:T(8,128)S(1)}, u32[]{:S(2)}, u32[]{:S(2)}) collective-permute-start(f32[8,640]{1,0:T(8,128)S(1)} %get-tuple-element.25), channel_id=1, source_target_pairs={{8,16},{16,8},{24,32},{32,24},{40,48},{48,40},{56,64},{64,56},{72,... | collective-permute-start | bytes 61448 | tf_op jit(solution)/shard_map/ppermute | solution.py:305
  18.2 19.0 %collective-permute-start.2 = (f32[8,640]{1,0:T(8,128)S(1)}, f32[8,640]{1,0:T(8,128)S(1)}, u32[]{:S(2)}, u32[]{:S(2)}) collective-permute-start(f32[8,640]{1,0:T(8,128)S(1)} %get-tuple-element.23), channel_id=1, source_target_pairs={{0,8},{8,0},{16,24},{24,16},{32,40},{40,32},{48,56},{56,48},{64,72... | collective-permute-start | bytes 61448 | tf_op jit(solution)/shard_map/ppermute | solution.py:306
  37.2 25.2 %copy-start = (f32[1,1,256,256]{3,2,1,0:T(8,128)S(1)}, f32[1,1,256,256]{3,2,1,0:T(8,128)}, u32[]{:S(2)}) copy-start(f32[1,1,256,256]{3,2,1,0:T(8,128)} %param.18) | copy-start | bytes 786436
  39.4 23.0 %copy-start.1 = (f32[32,32]{1,0:T(8,128)S(1)}, f32[32,32]{1,0:T(8,128)}, u32[]{:S(2)}) copy-start(f32[32,32]{1,0:T(8,128)} %sub_ref.1) | copy-start | bytes 12292

commit v4 on v3

--- a/solution.py
+++ b/solution.py
@@ -110,14 +110,17 @@
     edge_ref[...] = pick_edges(edge_columns(height_ref[...], wet_depth).T)
 
 
-def rims(parity_lat, ra, rb):
-    south = jnp.where(parity_lat == 0, ra, rb)
-    north = jnp.where(parity_lat == 0, rb, ra)
-    return north, south
-
-
-def corners(par_ref, edge_ref, ra_ref, rb_ref, first_ref, second_ref, block_ref):
-    north, south = rims(par_ref[1], ra_ref[...], rb_ref[...])
+def is_even(axis):
+    return (lax.axis_index(axis) & 1) == 0
+
+
+def rims(ra, rb):
+    even = is_even("lat")
+    return jnp.where(even, rb, ra), jnp.where(even, ra, rb)
+
+
+def corners(edge_ref, ra_ref, rb_ref, first_ref, second_ref, block_ref):
+    north, south = rims(ra_ref[...], rb_ref[...])
     block = join_rows(
         edge_columns(south[0:8], south[8:16]),
         jnp.zeros((LANES - 16, LANES), F32),
@@ -128,8 +131,9 @@
     strips = join_cols(edge_ref[...], block)
     west = join_rows(strips[0:RIM], strips[EDGE:EDGE + RIM])
     east = join_rows(strips[4 * EDGE - RIM:], strips[3 * EDGE - RIM:3 * EDGE])
-    first_ref[...] = jnp.where(par_ref[0] == 0, east, west)
-    second_ref[...] = jnp.where(par_ref[0] == 0, west, east)
+    even = is_even("lon")
+    first_ref[...] = jnp.where(even, east, west)
+    second_ref[...] = jnp.where(even, west, east)
 
 
 def march(height, wet_depth, right, below):
@@ -151,18 +155,19 @@
     return height
 
 
-def inner(par_ref, height_ref, wet_depth_ref, ra_ref, rb_ref, out_ref):
-    north, south = rims(par_ref[1], ra_ref[...], rb_ref[...])
+def inner(height_ref, wet_depth_ref, ra_ref, rb_ref, out_ref):
+    north, south = rims(ra_ref[...], rb_ref[...])
     height = join_rows(north[0:8], height_ref[...], south[0:8])
     wet_depth = join_rows(north[8:16], wet_depth_ref[...], south[8:16])
     out_ref[...] = march(height, wet_depth, 1, 0)[8:8 + out_ref.shape[0]]
 
 
-def forward(par_ref, inner_ref, edge_ref, block_ref, ea_ref, eb_ref, lat4_ref, lon_t_ref,
-            hot_ref, mask_ref, out_ref, send_ref, final_buf, sem):
+def forward(inner_ref, edge_ref, block_ref, ea_ref, eb_ref, lat4_ref, lon_t_ref,
+            hot_ref, mask_ref, final_ref, send_ref):
     rows_own = inner_ref.shape[0]
-    from_east = jnp.where(par_ref[0] == 0, ea_ref[...], eb_ref[...])
-    from_west = jnp.where(par_ref[0] == 0, eb_ref[...], ea_ref[...])
+    even = is_even("lon")
+    from_east = jnp.where(even, ea_ref[...], eb_ref[...])
+    from_west = jnp.where(even, eb_ref[...], ea_ref[...])
     own = join_cols(edge_ref[...], block_ref[...])
     strip = march(
         join_rows(from_west[0:RIM], own[0:EDGE], own[3 * EDGE:], from_east[0:RIM]),
@@ -174,9 +179,7 @@
     ).T
     lane = iota((rows_own, LANES), 1)
     final = jnp.where((lane < RIM) | (lane >= LANES - RIM), table, inner_ref[...])
-    final_buf[...] = final
-    write = pltpu.make_async_copy(final_buf, out_ref, sem)
-    write.start()
+    final_ref[...] = final
 
     high, low = parts(final)
     lon_high, lon_low = lon_t_ref[:LANES, :], lon_t_ref[LANES:, :]
@@ -196,10 +199,11 @@
     mask = mask_ref[...]
     filled = jnp.where(iota(mask.shape, 1) < CAP * SUB, values * mask, mask)
     send_ref[...] = fold(dot(hot_ref[...], join_cols(*parts(filled))))
-    write.wait()
-
-
-def smooth(recv_ref, prior_ref, sub_ref, reply_ref):
+
+
+def smooth(recv_ref, prior_ref, sub_ref, final_ref, reply_ref, out_ref, sem):
+    write = pltpu.make_async_copy(final_ref, out_ref, sem)
+    write.start()
     received = recv_ref[...]
     turned = received.T
     devices = received.shape[0]
@@ -232,6 +236,7 @@
         found = fold(dot(member, both))
         reply = found if reply is None else jnp.where(group == r, found, reply)
     reply_ref[...] = reply
+    write.wait()
 
 
 def backward(ret_ref, hot_t_ref, mask_ref, lat4_ref, lon_ref, out_ref, buf, sems):
@@ -268,7 +273,6 @@
 
 
 VMEM = pl.BlockSpec(memory_space=pltpu.VMEM)
-SMEM = pl.BlockSpec(memory_space=pltpu.SMEM)
 HBM = pl.BlockSpec(memory_space=pltpu.HBM)
 
 
@@ -297,13 +301,9 @@
 
 
 def swap(payload, axis, periodic):
-    if axis == "lat":
-        second = lax.ppermute(payload[1], axis, swap_pairs(axis, 1, periodic))
-        late, _ = lax.optimization_barrier((payload[0], payload[1]))
-        return lax.ppermute(late, axis, swap_pairs(axis, 0, periodic)), second
-    late, _ = lax.optimization_barrier((payload[1], payload[0]))
-    second = lax.ppermute(late, axis, swap_pairs(axis, 1, periodic))
-    return lax.ppermute(payload[0], axis, swap_pairs(axis, 0, periodic)), second
+    far, _ = lax.optimization_barrier((payload[1], payload[0]))
+    far = lax.ppermute(far, axis, swap_pairs(axis, 1, periodic))
+    return lax.ppermute(payload[0], axis, swap_pairs(axis, 0, periodic)), far
 
 
 def local(
@@ -321,14 +321,13 @@
     rows, cols = adjoint_height.shape
     lon_devices = lax.axis_size("lon")
     total = (rows // TS) * (cols // TS)
-    parity = jnp.stack([lax.axis_index("lon") & 1, lax.axis_index("lat") & 1]).astype(jnp.int32)
 
     def edge_rows(start):
         def cut(x):
             return lax.dynamic_slice_in_dim(x, start, 8, axis=0)
         return jnp.concatenate([cut(adjoint_height), cut(depth) * cut(wet).astype(F32)], axis=0)
 
-    last = (rows - 8) * (1 - parity[1])
+    last = (rows - 8) * (1 - (lax.axis_index("lat") & 1))
     north_a, north_b = swap([edge_rows(last), edge_rows(rows - 8 - last)], "lat", False)
     dma = pltpu.SemaphoreType.DMA
     own = pltpu.VMEM((rows, cols), F32)
@@ -358,28 +357,28 @@
     payload = ((2 * RIM, rows + LANES), F32, VMEM)
     first, second, block = call(
         corners,
-        [SMEM] + [VMEM] * 3,
+        [VMEM] * 3,
         [payload, payload, ((4 * EDGE, LANES), F32, VMEM)],
-        parity, edges, north_a, north_b,
+        edges, north_a, north_b,
     )
     east_a, east_b = swap([first, second], "lon", True)
     (middle,) = call(
-        inner, [SMEM] + [VMEM] * 4, [((rows, cols), F32, VMEM)],
-        parity, height, wet_depth, north_a, north_b,
-    )
-    final, sent = call(
+        inner, [VMEM] * 4, [((rows, cols), F32, VMEM)],
+        height, wet_depth, north_a, north_b,
+    )
+    ended, sent = call(
         forward,
-        [SMEM] + [VMEM] * 9,
-        [((rows, cols), F32, HBM), ((lon_devices, LANES), F32, VMEM)],
-        parity, middle, edges, block, east_a, east_b, lat4, lon_t, hot, mask,
-        scratch=[own, dma(())],
+        [VMEM] * 9,
+        [((rows, cols), F32, VMEM), ((lon_devices, LANES), F32, VMEM)],
+        middle, edges, block, east_a, east_b, lat4, lon_t, hot, mask,
     )
     received = lax.all_to_all(sent, "lon", split_axis=0, concat_axis=0, tiled=True)
-    (replies,) = call(
+    replies, final = call(
         smooth,
-        [VMEM] * 3,
-        [((lon_devices, LANES), F32, VMEM)],
-        received, prior_patches.reshape(NPATCH, NPATCH), prior_subfaults,
+        [VMEM] * 4,
+        [((lon_devices, LANES), F32, VMEM), ((rows, cols), F32, HBM)],
+        received, prior_patches.reshape(NPATCH, NPATCH), prior_subfaults, ended,
+        scratch=[dma(())],
     )
     returned = lax.all_to_all(replies, "lon", split_axis=0, concat_axis=0, tiled=True)
     (gradient,) = call(

time: 85.1 us -> 83.3 us (0.979)
  Pallas kernels: 8.51 us -> 6.69 us
    pallas_call x6, Pallas kernels: 8.51 us -> 6.69 us  [call(): pl.pallas_call(kernel, out_shape=[jax.ShapeDtypeStruct(shape, dtype) for...]
  transfers between devices with their start and end apart: 4 -> 4, of which waited for: 1 -> 1; matrix products, arithmetic and copies ran while one was open for 0% -> 0% of each run, Pallas kernels for 4% -> 3%
where the time goes in v4:
time: 83.3 us; the launch traced here: 82.9 us
  blocking collectives  43 us (52%)
  starting transfers between devices  31.2 us (37%)
  Pallas kernels  6.69 us (8%)
    all_to_all x1, blocking collectives, local(): lax.all_to_all(sent, 'lon', split_axis=0, concat_axis=0, tiled=True)  23 us
    all_to_all x1, blocking collectives, local(): lax.all_to_all(replies, 'lon', split_axis=0, concat_axis=0, tiled=True)  20 us
    ppermute x2, starting transfers between devices, swap(): return (lax.ppermute(payload[0], axis, swap_pairs(axis, 0, periodic)), far)  19.6 us
    ppermute x2, starting transfers between devices, swap(): far = lax.ppermute(far, axis, swap_pairs(axis, 1, periodic))  11.6 us
    pallas_call x6, Pallas kernels, call(): pl.pallas_call(kernel, out_shape=[jax.ShapeDtypeStruct(shape, dtype) for...  6.69 us
  transfers between devices with their start and end apart: 4, of which 1 were waited for; matrix products, arithmetic and copies ran while one was open for 0% of the time, Pallas kernels for 3%

profile of v4, /device:TPU:7, one launch (start us, length us, event | category | flops | bytes accessed | tf_op | source)
XLA Modules:
  0.0 82.9 jit_solution(3698814322551534780)
XLA Ops:
  0.6 0.8 convert_multiply_fusion
  1.4 7.4 %collective-permute-start.1 = (f32[16,128]{1,0:T(8,128)S(1)}, f32[16,128]{1,0:T(8,128)S(1)}, u32[]{:S(2)}, u32[]{:S(2)}) collective-permute-start(f32[16,128]{1,0:T(8,128)S(1)} %pad_maximum_fusion.1), channel_id=1, source_target_pairs={{1,2},{2,1},{3,4},{4,3},{5,6},{6,5},{9,10},{10,9},{11,12},{12,11},... | collective-permute-start | bytes 24584 | tf_op jit(solution)/shard_map/ppermute | solution.py:305
  8.8 1.9 %collective-permute-start = (f32[16,128]{1,0:T(8,128)S(1)}, f32[16,128]{1,0:T(8,128)S(1)}, u32[]{:S(2)}, u32[]{:S(2)}) collective-permute-start(f32[16,128]{1,0:T(8,128)S(1)} %pad_maximum_fusion), channel_id=1, source_target_pairs={{0,1},{1,0},{2,3},{3,2},{4,5},{5,4},{6,7},{7,6},{8,9},{9,8},{10,11... | collective-permute-start | bytes 24584 | tf_op jit(solution)/shard_map/ppermute | solution.py:306
  10.7 2.0 %shard_map.113 = (f32[512,128]{1,0:T(8,128)S(1)}, f32[512,128]{1,0:T(8,128)S(1)}, f32[32,512]{1,0:T(8,128)S(1)}, f32[512,128]{1,0:T(8,128)S(1)}, bf16[256,256]{1...) custom-call(f32[32,512]{1,0:T(8,128)} %lat_hbm.1, ...), custom_call_target="tpu_custom_call" | custom-call | tf_op jit(solution)/shard_map/pallas_call | solution.py:280
  12.8 0.0 collective-permute-done.1.rb_ref
  12.8 0.5 collective-permute-done.ra_ref
  13.3 0.2 shard_map.115
  13.4 4.2 %collective-permute-start.3 = (f32[8,640]{1,0:T(8,128)S(1)}, f32[8,640]{1,0:T(8,128)S(1)}, u32[]{:S(2)}, u32[]{:S(2)}) collective-permute-start(f32[8,640]{1,0:T(8,128)S(1)} %get-tuple-element.27), channel_id=1, source_target_pairs={{8,16},{16,8},{24,32},{32,24},{40,48},{48,40},{56,64},{64,56},{72,... | collective-permute-start | bytes 61448 | tf_op jit(solution)/shard_map/ppermute | solution.py:305
  17.7 17.6 %collective-permute-start.2 = (f32[8,640]{1,0:T(8,128)S(1)}, f32[8,640]{1,0:T(8,128)S(1)}, u32[]{:S(2)}, u32[]{:S(2)}) collective-permute-start(f32[8,640]{1,0:T(8,128)S(1)} %get-tuple-element.25), channel_id=1, source_target_pairs={{0,8},{8,0},{16,24},{24,16},{32,40},{40,32},{48,56},{56,48},{64,72... | collective-permute-start | bytes 61448 | tf_op jit(solution)/shard_map/ppermute | solution.py:306
  35.3 0.8 shard_map.114.inner_ref
  36.1 0.0 collective-permute-done.3.eb_ref
  36.1 0.0 collective-permute-done.2.ea_ref
  36.1 0.0 copy-start
  36.1 1.4 %shard_map.116 = (f32[512,128]{1,0:T(8,128)S(1)}, f32[128,128]{1,0:T(8,128)S(1)}) custom-call(f32[512,128]{1,0:T(8,128)S(1)} %shard_map.114.inner_ref, f32[32,512]{1,0:T(8,128)S(1)} %get-tuple-element.23.edge_ref, f32[32,128]{1,0:T(8,128)S(1)} %get-tuple-element.24.block_ref, f32[8,640]{1,0:T(8,128)S(1)} %collective-permute-done.2.ea_ref, ...), custom_call_target="tpu_custom_call" | custom-call | tf_op jit(solution)/shard_map/pallas_call | solution.py:280
  37.6 0.0 copy-start.1
  37.6 23.0 %all_to_all.22 = f32[128,1,128]{2,1,0:T(1,128)S(1)} all-to-all(f32[128,1,128]{2,1,0:T(1,128)S(1)} %bitcast.15), channel_id=1, replica_groups=mesh['lon'=128,'lat'=8] {'lon'}, dimensions={0} | all-to-all | bytes 131072 | tf_op jit(solution)/shard_map/all_to_all | solution.py:375
  60.6 0.0 copy-done
  60.6 0.0 copy-done.1
  60.6 1.0 %shard_map.117 = (f32[128,128]{1,0:T(8,128)S(1)}, f32[512,128]{1,0:T(8,128)}) custom-call(f32[128,128]{1,0:T(8,128)S(1)} %bitcast.13, f32[256,256]{1,0:T(8,128)S(1)} %bitcast.12, f32[32,32]{1,0:T(8,128)S(1)} %copy-done.1, f32[512,128]{1,0:T(8,128)S(1)} %get-tuple-element.33.final_ref), custom_call_target="tpu_custom_call" | custom-call | tf_op jit(solution)/shard_map/pallas_call | solution.py:280
  61.6 20.0 %all_to_all.23 = f32[128,1,128]{2,1,0:T(1,128)S(1)} all-to-all(f32[128,1,128]{2,1,0:T(1,128)S(1)} %bitcast.16), channel_id=1, replica_groups=mesh['lon'=128,'lat'=8] {'lon'}, dimensions={0} | all-to-all | bytes 131072 | tf_op jit(solution)/shard_map/all_to_all | solution.py:383
  81.6 1.4 %shard_map.118 = f32[512,128]{1,0:T(8,128)} custom-call(f32[128,128]{1,0:T(8,128)S(1)} %bitcast.14, bf16[256,256]{1,0:T(8,128)(2,1)S(1)} %get-tuple-element.36.hot_t_ref, f32[256,128]{1,0:T(8,128)S(1)} %get-tuple-element.31.mask_ref, f32[512,128]{1,0:T(8,128)S(1)} %get-tuple-element.28.lat4_ref, bf16[256,256]{1,0:T(8,128)(2,1)S(1)} %get-tuple-element.37.lon_ref), custom_call_target="tpu_custom_call" | custom-call | tf_op jit(solution)/shard_map/pallas_call | solution.py:280
  (2 shorter events, 0.0 us)
Async XLA Ops:
  1.4 11.3 %collective-permute-start.1 = (f32[16,128]{1,0:T(8,128)S(1)}, f32[16,128]{1,0:T(8,128)S(1)}, u32[]{:S(2)}, u32[]{:S(2)}) collective-permute-start(f32[16,128]{1,0:T(8,128)S(1)} %pad_maximum_fusion.1), channel_id=1, source_target_pairs={{1,2},{2,1},{3,4},{4,3},{5,6},{6,5},{9,10},{10,9},{11,12},{12,11},... | collective-permute-start | bytes 24584 | tf_op jit(solution)/shard_map/ppermute | solution.py:305
  8.8 4.5 %collective-permute-start = (f32[16,128]{1,0:T(8,128)S(1)}, f32[16,128]{1,0:T(8,128)S(1)}, u32[]{:S(2)}, u32[]{:S(2)}) collective-permute-start(f32[16,128]{1,0:T(8,128)S(1)} %pad_maximum_fusion), channel_id=1, source_target_pairs={{0,1},{1,0},{2,3},{3,2},{4,5},{5,4},{6,7},{7,6},{8,9},{9,8},{10,11... | collective-permute-start | bytes 24584 | tf_op jit(solution)/shard_map/ppermute | solution.py:306
  13.4 22.7 %collective-permute-start.3 = (f32[8,640]{1,0:T(8,128)S(1)}, f32[8,640]{1,0:T(8,128)S(1)}, u32[]{:S(2)}, u32[]{:S(2)}) collective-permute-start(f32[8,640]{1,0:T(8,128)S(1)} %get-tuple-element.27), channel_id=1, source_target_pairs={{8,16},{16,8},{24,32},{32,24},{40,48},{48,40},{56,64},{64,56},{72,... | collective-permute-start | bytes 61448 | tf_op jit(solution)/shard_map/ppermute | solution.py:305
  17.7 18.5 %collective-permute-start.2 = (f32[8,640]{1,0:T(8,128)S(1)}, f32[8,640]{1,0:T(8,128)S(1)}, u32[]{:S(2)}, u32[]{:S(2)}) collective-permute-start(f32[8,640]{1,0:T(8,128)S(1)} %get-tuple-element.25), channel_id=1, source_target_pairs={{0,8},{8,0},{16,24},{24,16},{32,40},{40,32},{48,56},{56,48},{64,72... | collective-permute-start | bytes 61448 | tf_op jit(solution)/shard_map/ppermute | solution.py:306
  36.1 24.5 %copy-start = (f32[1,1,256,256]{3,2,1,0:T(8,128)S(1)}, f32[1,1,256,256]{3,2,1,0:T(8,128)}, u32[]{:S(2)}) copy-start(f32[1,1,256,256]{3,2,1,0:T(8,128)} %param.18) | copy-start | bytes 786436
  37.6 23.0 %copy-start.1 = (f32[32,32]{1,0:T(8,128)S(1)}, f32[32,32]{1,0:T(8,128)}, u32[]{:S(2)}) copy-start(f32[32,32]{1,0:T(8,128)} %sub_ref.1) | copy-start | bytes 12292

commit v5 on v4

--- a/solution.py
+++ b/solution.py
@@ -12,7 +12,8 @@
 NPATCH = 256
 CAP = 3
 EDGE = 8
-WRITES = 4
+WRITES = 2
+CHUNKS = 4
 COURANT = 0.6
 LANES = 128
 F32 = jnp.float32
@@ -177,17 +178,21 @@
     table = join_rows(
         strip[RIM:2 * RIM], jnp.zeros((LANES - 2 * RIM, rows_own), F32), strip[2 * EDGE:2 * EDGE + RIM]
     ).T
-    lane = iota((rows_own, LANES), 1)
-    final = jnp.where((lane < RIM) | (lane >= LANES - RIM), table, inner_ref[...])
-    final_ref[...] = final
-
-    high, low = parts(final)
     lon_high, lon_low = lon_t_ref[:LANES, :], lon_t_ref[LANES:, :]
-    product = dot(join_cols(high, low), join_rows(lon_high, lon_high)) + dot(high, lon_low)
-    lat4 = lat4_ref[...]
-    product = product * join_cols(lat4, lat4)
+    lon_both = join_rows(lon_high, lon_high)
     tile_rows = rows_own // TS
-    sums = jnp.sum(product.reshape(tile_rows, TS, product.shape[1]), axis=1)
+    share = rows_own // CHUNKS
+    lane = iota((share, LANES), 1)
+    pieces = []
+    for i in range(CHUNKS):
+        span = slice(i * share, (i + 1) * share)
+        final = jnp.where((lane < RIM) | (lane >= LANES - RIM), table[span], inner_ref[span, :])
+        final_ref[span, :] = final
+        high, low = parts(final)
+        lat4 = lat4_ref[span, :]
+        product = (dot(join_cols(high, low), lon_both) + dot(high, lon_low)) * join_cols(lat4, lat4)
+        pieces.append(jnp.sum(product.reshape(share // TS, TS, product.shape[1]), axis=1))
+    sums = join_rows(*pieces)
     group = iota((tile_rows, LANES), 1) // SUB
     stacked = []
     for q in range(sums.shape[1] // LANES):

time: 83.3 us -> 83.1 us (level)
  no operation moved by 1% of the time
where the time goes in v5:
time: 83.1 us; the launch traced here: 82.7 us
  blocking collectives  43 us (52%)
  starting transfers between devices  31.2 us (38%)
  Pallas kernels  6.51 us (8%)
    all_to_all x1, blocking collectives, local(): lax.all_to_all(sent, 'lon', split_axis=0, concat_axis=0, tiled=True)  23 us
    all_to_all x1, blocking collectives, local(): lax.all_to_all(replies, 'lon', split_axis=0, concat_axis=0, tiled=True)  20 us
    ppermute x2, starting transfers between devices, swap(): return (lax.ppermute(payload[0], axis, swap_pairs(axis, 0, periodic)), far)  19.6 us
    ppermute x2, starting transfers between devices, swap(): far = lax.ppermute(far, axis, swap_pairs(axis, 1, periodic))  11.6 us
    pallas_call x6, Pallas kernels, call(): pl.pallas_call(kernel, out_shape=[jax.ShapeDtypeStruct(shape, dtype) for...  6.51 us
  transfers between devices with their start and end apart: 4, of which 1 were waited for; matrix products, arithmetic and copies ran while one was open for 0% of the time, Pallas kernels for 3%

profile of v5, /device:TPU:7, one launch (start us, length us, event | category | flops | bytes accessed | tf_op | source)
XLA Modules:
  0.0 82.7 jit_solution(17033296000329100710)
XLA Ops:
  0.6 0.8 convert_multiply_fusion
  1.4 7.4 %collective-permute-start.1 = (f32[16,128]{1,0:T(8,128)S(1)}, f32[16,128]{1,0:T(8,128)S(1)}, u32[]{:S(2)}, u32[]{:S(2)}) collective-permute-start(f32[16,128]{1,0:T(8,128)S(1)} %pad_maximum_fusion.1), channel_id=1, source_target_pairs={{1,2},{2,1},{3,4},{4,3},{5,6},{6,5},{9,10},{10,9},{11,12},{12,11},... | collective-permute-start | bytes 24584 | tf_op jit(solution)/shard_map/ppermute | solution.py:310
  8.8 1.9 %collective-permute-start = (f32[16,128]{1,0:T(8,128)S(1)}, f32[16,128]{1,0:T(8,128)S(1)}, u32[]{:S(2)}, u32[]{:S(2)}) collective-permute-start(f32[16,128]{1,0:T(8,128)S(1)} %pad_maximum_fusion), channel_id=1, source_target_pairs={{0,1},{1,0},{2,3},{3,2},{4,5},{5,4},{6,7},{7,6},{8,9},{9,8},{10,11... | collective-permute-start | bytes 24584 | tf_op jit(solution)/shard_map/ppermute | solution.py:311
  10.7 2.0 %shard_map.113 = (f32[512,128]{1,0:T(8,128)S(1)}, f32[512,128]{1,0:T(8,128)S(1)}, f32[32,512]{1,0:T(8,128)S(1)}, f32[512,128]{1,0:T(8,128)S(1)}, bf16[256,256]{1...) custom-call(f32[32,512]{1,0:T(8,128)} %lat_hbm.1, ...), custom_call_target="tpu_custom_call" | custom-call | tf_op jit(solution)/shard_map/pallas_call | solution.py:285
  12.8 0.0 collective-permute-done.1.rb_ref
  12.8 0.5 collective-permute-done.ra_ref
  13.3 0.2 shard_map.115
  13.4 4.2 %collective-permute-start.3 = (f32[8,640]{1,0:T(8,128)S(1)}, f32[8,640]{1,0:T(8,128)S(1)}, u32[]{:S(2)}, u32[]{:S(2)}) collective-permute-start(f32[8,640]{1,0:T(8,128)S(1)} %get-tuple-element.27), channel_id=1, source_target_pairs={{8,16},{16,8},{24,32},{32,24},{40,48},{48,40},{56,64},{64,56},{72,... | collective-permute-start | bytes 61448 | tf_op jit(solution)/shard_map/ppermute | solution.py:310
  17.7 17.6 %collective-permute-start.2 = (f32[8,640]{1,0:T(8,128)S(1)}, f32[8,640]{1,0:T(8,128)S(1)}, u32[]{:S(2)}, u32[]{:S(2)}) collective-permute-start(f32[8,640]{1,0:T(8,128)S(1)} %get-tuple-element.25), channel_id=1, source_target_pairs={{0,8},{8,0},{16,24},{24,16},{32,40},{40,32},{48,56},{56,48},{64,72... | collective-permute-start | bytes 61448 | tf_op jit(solution)/shard_map/ppermute | solution.py:311
  35.3 0.8 shard_map.114.inner_ref
  36.1 0.0 collective-permute-done.3.eb_ref
  36.1 0.0 collective-permute-done.2.ea_ref
  36.1 0.0 copy-start
  36.1 1.3 %shard_map.116 = (f32[512,128]{1,0:T(8,128)S(1)}, f32[128,128]{1,0:T(8,128)S(1)}) custom-call(f32[512,128]{1,0:T(8,128)S(1)} %shard_map.114.inner_ref, f32[32,512]{1,0:T(8,128)S(1)} %get-tuple-element.23.edge_ref, f32[32,128]{1,0:T(8,128)S(1)} %get-tuple-element.24.block_ref, f32[8,640]{1,0:T(8,128)S(1)} %collective-permute-done.2.ea_ref, ...), custom_call_target="tpu_custom_call" | custom-call | tf_op jit(solution)/shard_map/pallas_call | solution.py:285
  37.4 0.0 copy-start.1
  37.5 23.0 %all_to_all.22 = f32[128,1,128]{2,1,0:T(1,128)S(1)} all-to-all(f32[128,1,128]{2,1,0:T(1,128)S(1)} %bitcast.15), channel_id=1, replica_groups=mesh['lon'=128,'lat'=8] {'lon'}, dimensions={0} | all-to-all | bytes 131072 | tf_op jit(solution)/shard_map/all_to_all | solution.py:380
  60.5 0.0 copy-done
  60.5 0.0 copy-done.1
  60.5 1.0 %shard_map.117 = (f32[128,128]{1,0:T(8,128)S(1)}, f32[512,128]{1,0:T(8,128)}) custom-call(f32[128,128]{1,0:T(8,128)S(1)} %bitcast.13, f32[256,256]{1,0:T(8,128)S(1)} %bitcast.12, f32[32,32]{1,0:T(8,128)S(1)} %copy-done.1, f32[512,128]{1,0:T(8,128)S(1)} %get-tuple-element.33.final_ref), custom_call_target="tpu_custom_call" | custom-call | tf_op jit(solution)/shard_map/pallas_call | solution.py:285
  61.4 20.0 %all_to_all.23 = f32[128,1,128]{2,1,0:T(1,128)S(1)} all-to-all(f32[128,1,128]{2,1,0:T(1,128)S(1)} %bitcast.16), channel_id=1, replica_groups=mesh['lon'=128,'lat'=8] {'lon'}, dimensions={0} | all-to-all | bytes 131072 | tf_op jit(solution)/shard_map/all_to_all | solution.py:388
  81.5 1.3 %shard_map.118 = f32[512,128]{1,0:T(8,128)} custom-call(f32[128,128]{1,0:T(8,128)S(1)} %bitcast.14, bf16[256,256]{1,0:T(8,128)(2,1)S(1)} %get-tuple-element.36.hot_t_ref, f32[256,128]{1,0:T(8,128)S(1)} %get-tuple-element.31.mask_ref, f32[512,128]{1,0:T(8,128)S(1)} %get-tuple-element.28.lat4_ref, bf16[256,256]{1,0:T(8,128)(2,1)S(1)} %get-tuple-element.37.lon_ref), custom_call_target="tpu_custom_call" | custom-call | tf_op jit(solution)/shard_map/pallas_call | solution.py:285
  (2 shorter events, 0.0 us)
Async XLA Ops:
  1.4 11.3 %collective-permute-start.1 = (f32[16,128]{1,0:T(8,128)S(1)}, f32[16,128]{1,0:T(8,128)S(1)}, u32[]{:S(2)}, u32[]{:S(2)}) collective-permute-start(f32[16,128]{1,0:T(8,128)S(1)} %pad_maximum_fusion.1), channel_id=1, source_target_pairs={{1,2},{2,1},{3,4},{4,3},{5,6},{6,5},{9,10},{10,9},{11,12},{12,11},... | collective-permute-start | bytes 24584 | tf_op jit(solution)/shard_map/ppermute | solution.py:310
  8.8 4.5 %collective-permute-start = (f32[16,128]{1,0:T(8,128)S(1)}, f32[16,128]{1,0:T(8,128)S(1)}, u32[]{:S(2)}, u32[]{:S(2)}) collective-permute-start(f32[16,128]{1,0:T(8,128)S(1)} %pad_maximum_fusion), channel_id=1, source_target_pairs={{0,1},{1,0},{2,3},{3,2},{4,5},{5,4},{6,7},{7,6},{8,9},{9,8},{10,11... | collective-permute-start | bytes 24584 | tf_op jit(solution)/shard_map/ppermute | solution.py:311
  13.4 22.7 %collective-permute-start.3 = (f32[8,640]{1,0:T(8,128)S(1)}, f32[8,640]{1,0:T(8,128)S(1)}, u32[]{:S(2)}, u32[]{:S(2)}) collective-permute-start(f32[8,640]{1,0:T(8,128)S(1)} %get-tuple-element.27), channel_id=1, source_target_pairs={{8,16},{16,8},{24,32},{32,24},{40,48},{48,40},{56,64},{64,56},{72,... | collective-permute-start | bytes 61448 | tf_op jit(solution)/shard_map/ppermute | solution.py:310
  17.7 18.5 %collective-permute-start.2 = (f32[8,640]{1,0:T(8,128)S(1)}, f32[8,640]{1,0:T(8,128)S(1)}, u32[]{:S(2)}, u32[]{:S(2)}) collective-permute-start(f32[8,640]{1,0:T(8,128)S(1)} %get-tuple-element.25), channel_id=1, source_target_pairs={{0,8},{8,0},{16,24},{24,16},{32,40},{40,32},{48,56},{56,48},{64,72... | collective-permute-start | bytes 61448 | tf_op jit(solution)/shard_map/ppermute | solution.py:311
  36.1 24.3 %copy-start = (f32[1,1,256,256]{3,2,1,0:T(8,128)S(1)}, f32[1,1,256,256]{3,2,1,0:T(8,128)}, u32[]{:S(2)}) copy-start(f32[1,1,256,256]{3,2,1,0:T(8,128)} %param.18) | copy-start | bytes 786436
  37.4 23.0 %copy-start.1 = (f32[32,32]{1,0:T(8,128)S(1)}, f32[32,32]{1,0:T(8,128)}, u32[]{:S(2)}) copy-start(f32[32,32]{1,0:T(8,128)} %sub_ref.1) | copy-start | bytes 12292

commit v6 on v5

--- a/solution.py
+++ b/solution.py
@@ -234,12 +234,14 @@
     smoothed = dot(join_cols(high, low), join_rows(sub_high, sub_high)) + dot(high, sub_low)
     both = join_cols(*parts(smoothed))
     group = iota((devices, LANES), 1) // SUB
-    reply = None
-    for r in range(CAP):
-        line = jnp.broadcast_to(received[:, CAP * SUB + r:CAP * SUB + r + 1], (devices, NPATCH))
-        member = (line == iota((devices, NPATCH), 1).astype(F32)).astype(BF16)
-        found = fold(dot(member, both))
-        reply = found if reply is None else jnp.where(group == r, found, reply)
+    numbers = join_rows(*[
+        jnp.broadcast_to(received[:, CAP * SUB + r:CAP * SUB + r + 1], (devices, NPATCH))
+        for r in range(CAP)
+    ])
+    found = fold(dot((numbers == iota(numbers.shape, 1).astype(F32)).astype(BF16), both))
+    reply = found[:devices]
+    for r in range(1, CAP):
+        reply = jnp.where(group == r, found[r * devices:(r + 1) * devices], reply)
     reply_ref[...] = reply
     write.wait()
 

time: 83.1 us -> 83.1 us (level)
  no operation moved by 1% of the time
where the time goes in v6:
time: 83.1 us; the launch traced here: 82.7 us
  blocking collectives  43 us (52%)
  starting transfers between devices  31.2 us (38%)
  Pallas kernels  6.5 us (8%)
    all_to_all x1, blocking collectives, local(): lax.all_to_all(sent, 'lon', split_axis=0, concat_axis=0, tiled=True)  23 us
    all_to_all x1, blocking collectives, local(): lax.all_to_all(replies, 'lon', split_axis=0, concat_axis=0, tiled=True)  20 us
    ppermute x2, starting transfers between devices, swap(): return (lax.ppermute(payload[0], axis, swap_pairs(axis, 0, periodic)), far)  19.6 us
    ppermute x2, starting transfers between devices, swap(): far = lax.ppermute(far, axis, swap_pairs(axis, 1, periodic))  11.6 us
    pallas_call x6, Pallas kernels, call(): pl.pallas_call(kernel, out_shape=[jax.ShapeDtypeStruct(shape, dtype) for...  6.5 us
  transfers between devices with their start and end apart: 4, of which 1 were waited for; matrix products, arithmetic and copies ran while one was open for 0% of the time, Pallas kernels for 3%

profile of v6, /device:TPU:7, one launch (start us, length us, event | category | flops | bytes accessed | tf_op | source)
XLA Modules:
  0.0 82.7 jit_solution(8858644947243283918)
XLA Ops:
  0.6 0.8 convert_multiply_fusion
  1.4 7.4 %collective-permute-start.1 = (f32[16,128]{1,0:T(8,128)S(1)}, f32[16,128]{1,0:T(8,128)S(1)}, u32[]{:S(2)}, u32[]{:S(2)}) collective-permute-start(f32[16,128]{1,0:T(8,128)S(1)} %pad_maximum_fusion.1), channel_id=1, source_target_pairs={{1,2},{2,1},{3,4},{4,3},{5,6},{6,5},{9,10},{10,9},{11,12},{12,11},... | collective-permute-start | bytes 24584 | tf_op jit(solution)/shard_map/ppermute | solution.py:312
  8.8 1.9 %collective-permute-start = (f32[16,128]{1,0:T(8,128)S(1)}, f32[16,128]{1,0:T(8,128)S(1)}, u32[]{:S(2)}, u32[]{:S(2)}) collective-permute-start(f32[16,128]{1,0:T(8,128)S(1)} %pad_maximum_fusion), channel_id=1, source_target_pairs={{0,1},{1,0},{2,3},{3,2},{4,5},{5,4},{6,7},{7,6},{8,9},{9,8},{10,11... | collective-permute-start | bytes 24584 | tf_op jit(solution)/shard_map/ppermute | solution.py:313
  10.7 2.0 %shard_map.113 = (f32[512,128]{1,0:T(8,128)S(1)}, f32[512,128]{1,0:T(8,128)S(1)}, f32[32,512]{1,0:T(8,128)S(1)}, f32[512,128]{1,0:T(8,128)S(1)}, bf16[256,256]{1...) custom-call(f32[32,512]{1,0:T(8,128)} %lat_hbm.1, ...), custom_call_target="tpu_custom_call" | custom-call | tf_op jit(solution)/shard_map/pallas_call | solution.py:287
  12.8 0.0 collective-permute-done.1.rb_ref
  12.8 0.5 collective-permute-done.ra_ref
  13.3 0.2 shard_map.115
  13.4 4.2 %collective-permute-start.3 = (f32[8,640]{1,0:T(8,128)S(1)}, f32[8,640]{1,0:T(8,128)S(1)}, u32[]{:S(2)}, u32[]{:S(2)}) collective-permute-start(f32[8,640]{1,0:T(8,128)S(1)} %get-tuple-element.27), channel_id=1, source_target_pairs={{8,16},{16,8},{24,32},{32,24},{40,48},{48,40},{56,64},{64,56},{72,... | collective-permute-start | bytes 61448 | tf_op jit(solution)/shard_map/ppermute | solution.py:312
  17.7 17.6 %collective-permute-start.2 = (f32[8,640]{1,0:T(8,128)S(1)}, f32[8,640]{1,0:T(8,128)S(1)}, u32[]{:S(2)}, u32[]{:S(2)}) collective-permute-start(f32[8,640]{1,0:T(8,128)S(1)} %get-tuple-element.25), channel_id=1, source_target_pairs={{0,8},{8,0},{16,24},{24,16},{32,40},{40,32},{48,56},{56,48},{64,72... | collective-permute-start | bytes 61448 | tf_op jit(solution)/shard_map/ppermute | solution.py:313
  35.3 0.8 shard_map.114.inner_ref
  36.1 0.0 collective-permute-done.3.eb_ref
  36.1 0.0 collective-permute-done.2.ea_ref
  36.1 0.0 copy-start
  36.1 1.3 %shard_map.116 = (f32[512,128]{1,0:T(8,128)S(1)}, f32[128,128]{1,0:T(8,128)S(1)}) custom-call(f32[512,128]{1,0:T(8,128)S(1)} %shard_map.114.inner_ref, f32[32,512]{1,0:T(8,128)S(1)} %get-tuple-element.23.edge_ref, f32[32,128]{1,0:T(8,128)S(1)} %get-tuple-element.24.block_ref, f32[8,640]{1,0:T(8,128)S(1)} %collective-permute-done.2.ea_ref, ...), custom_call_target="tpu_custom_call" | custom-call | tf_op jit(solution)/shard_map/pallas_call | solution.py:287
  37.4 0.0 copy-start.1
  37.5 23.0 %all_to_all.22 = f32[128,1,128]{2,1,0:T(1,128)S(1)} all-to-all(f32[128,1,128]{2,1,0:T(1,128)S(1)} %bitcast.15), channel_id=1, replica_groups=mesh['lon'=128,'lat'=8] {'lon'}, dimensions={0} | all-to-all | bytes 131072 | tf_op jit(solution)/shard_map/all_to_all | solution.py:382
  60.5 0.0 copy-done
  60.5 0.0 copy-done.1
  60.5 0.9 %shard_map.117 = (f32[128,128]{1,0:T(8,128)S(1)}, f32[512,128]{1,0:T(8,128)}) custom-call(f32[128,128]{1,0:T(8,128)S(1)} %bitcast.13, f32[256,256]{1,0:T(8,128)S(1)} %bitcast.12, f32[32,32]{1,0:T(8,128)S(1)} %copy-done.1, f32[512,128]{1,0:T(8,128)S(1)} %get-tuple-element.33.final_ref), custom_call_target="tpu_custom_call" | custom-call | tf_op jit(solution)/shard_map/pallas_call | solution.py:287
  61.4 20.0 %all_to_all.23 = f32[128,1,128]{2,1,0:T(1,128)S(1)} all-to-all(f32[128,1,128]{2,1,0:T(1,128)S(1)} %bitcast.16), channel_id=1, replica_groups=mesh['lon'=128,'lat'=8] {'lon'}, dimensions={0} | all-to-all | bytes 131072 | tf_op jit(solution)/shard_map/all_to_all | solution.py:390
  81.5 1.3 %shard_map.118 = f32[512,128]{1,0:T(8,128)} custom-call(f32[128,128]{1,0:T(8,128)S(1)} %bitcast.14, bf16[256,256]{1,0:T(8,128)(2,1)S(1)} %get-tuple-element.36.hot_t_ref, f32[256,128]{1,0:T(8,128)S(1)} %get-tuple-element.31.mask_ref, f32[512,128]{1,0:T(8,128)S(1)} %get-tuple-element.28.lat4_ref, bf16[256,256]{1,0:T(8,128)(2,1)S(1)} %get-tuple-element.37.lon_ref), custom_call_target="tpu_custom_call" | custom-call | tf_op jit(solution)/shard_map/pallas_call | solution.py:287
  (2 shorter events, 0.0 us)
Async XLA Ops:
  1.4 11.3 %collective-permute-start.1 = (f32[16,128]{1,0:T(8,128)S(1)}, f32[16,128]{1,0:T(8,128)S(1)}, u32[]{:S(2)}, u32[]{:S(2)}) collective-permute-start(f32[16,128]{1,0:T(8,128)S(1)} %pad_maximum_fusion.1), channel_id=1, source_target_pairs={{1,2},{2,1},{3,4},{4,3},{5,6},{6,5},{9,10},{10,9},{11,12},{12,11},... | collective-permute-start | bytes 24584 | tf_op jit(solution)/shard_map/ppermute | solution.py:312
  8.8 4.5 %collective-permute-start = (f32[16,128]{1,0:T(8,128)S(1)}, f32[16,128]{1,0:T(8,128)S(1)}, u32[]{:S(2)}, u32[]{:S(2)}) collective-permute-start(f32[16,128]{1,0:T(8,128)S(1)} %pad_maximum_fusion), channel_id=1, source_target_pairs={{0,1},{1,0},{2,3},{3,2},{4,5},{5,4},{6,7},{7,6},{8,9},{9,8},{10,11... | collective-permute-start | bytes 24584 | tf_op jit(solution)/shard_map/ppermute | solution.py:313
  13.4 22.7 %collective-permute-start.3 = (f32[8,640]{1,0:T(8,128)S(1)}, f32[8,640]{1,0:T(8,128)S(1)}, u32[]{:S(2)}, u32[]{:S(2)}) collective-permute-start(f32[8,640]{1,0:T(8,128)S(1)} %get-tuple-element.27), channel_id=1, source_target_pairs={{8,16},{16,8},{24,32},{32,24},{40,48},{48,40},{56,64},{64,56},{72,... | collective-permute-start | bytes 61448 | tf_op jit(solution)/shard_map/ppermute | solution.py:312
  17.7 18.5 %collective-permute-start.2 = (f32[8,640]{1,0:T(8,128)S(1)}, f32[8,640]{1,0:T(8,128)S(1)}, u32[]{:S(2)}, u32[]{:S(2)}) collective-permute-start(f32[8,640]{1,0:T(8,128)S(1)} %get-tuple-element.25), channel_id=1, source_target_pairs={{0,8},{8,0},{16,24},{24,16},{32,40},{40,32},{48,56},{56,48},{64,72... | collective-permute-start | bytes 61448 | tf_op jit(solution)/shard_map/ppermute | solution.py:313
  36.1 24.3 %copy-start = (f32[1,1,256,256]{3,2,1,0:T(8,128)S(1)}, f32[1,1,256,256]{3,2,1,0:T(8,128)}, u32[]{:S(2)}) copy-start(f32[1,1,256,256]{3,2,1,0:T(8,128)} %param.18) | copy-start | bytes 786436
  37.4 23.0 %copy-start.1 = (f32[32,32]{1,0:T(8,128)S(1)}, f32[32,32]{1,0:T(8,128)}, u32[]{:S(2)}) copy-start(f32[32,32]{1,0:T(8,128)} %sub_ref.1) | copy-start | bytes 12292
